TPU v7x, 32 devices: a whole 2x2x4 slice. The times are simulated.
32 devices in a mesh: groups: 2 (over x), rows: 16 (over z, y, core).
Axes of the slice: x: 2, y: 2, z: 4, core: 2. Of those that a mesh axis runs over, the one named last changes fastest.
Arguments:
- in_acts: bfloat16 [512, 14336], P(('groups', 'rows')), parts along dimension 0, may hold values from -6 to 6
- out_grads: bfloat16 [512, 4096], P(('groups', 'rows')), parts along dimension 0, may hold values from -6 to 6
- in_projection: bfloat16 [128, 14336], replicated, may hold values from -0.046875 to 0.046875
- out_projection: bfloat16 [128, 4096], replicated, may hold values from -0.09375 to 0.09375
- inverse: bfloat16 [16384, 16384], P('rows'), as said below
- stored_rows: bfloat16 [1536, 16384], P(('groups', 'rows')), parts along dimension 0, may hold values from -0.0078125 to 0.0078125
- query_ids: int32 [512], P(('groups', 'rows')), parts along dimension 0, may hold values from 0 to 15, never falling along the last dimension, each value on 1 to 32 neighbouring positions
- example_ids: int32 [32, 48], P(('groups', 'rows')), parts along dimension 0, may hold values from 0 to 15, never falling along the last dimension, each value on 1 to 8 neighbouring positions
Outputs:
- example_scores: float32 [512, 16], P(('groups', 'rows')), parts along dimension 0
There are 2 independent parts, one for each index of `groups`. A program takes and returns all parts, laid end to end along the dimension named above; an argument that names none is the same for every part. Nothing has to cross between parts.
Inputs may be any that keep to these rules, and one draw needn't show every extreme that they name: `query_ids`: tokens of one query stand together, queries in increasing order; a query may span several devices. `example_ids`: within each block, rows of one example stand together in increasing order, each example with at least one row. `inverse`: the matrix is exactly symmetric.
All inputs are finite; a program needn't handle non-finite values.
Results may differ from a plain program's by a relative error of at most 0.0057.
Values may be sent and summed in bfloat16 or wider, within the bound.
No kernel may reach another device: no remote copies, remote signals or barrier semaphores. Data moves between devices by JAX's collectives and lax.ppermute only.
A program may use at most 128 MiB of HBM per device.

v0:
```python
import jax
import jax.numpy as jnp
from jax import lax
from jax.sharding import PartitionSpec as P

KIN = 128
KOUT = 128
QRY_DEV = 1
EX_DEV = 16


def on_device(
    in_acts, out_grads, in_projection, out_projection, inverse, stored_rows, query_ids, example_ids
):
    group_size = lax.axis_size("rows")
    queries = QRY_DEV * group_size
    tokens_here = in_acts.shape[0]
    owned_count = KOUT // group_size
    in_proj = lax.dot_general(
        in_acts, in_projection, (((1,), (1,)), ((), ())), preferred_element_type=jnp.float32
    ).astype(jnp.bfloat16)
    out_proj = lax.dot_general(
        out_grads, out_projection, (((1,), (1,)), ((), ())), preferred_element_type=jnp.float32
    ).astype(jnp.bfloat16)
    member = (query_ids[:, None] == jnp.arange(queries, dtype=jnp.int32)[None, :]).astype(
        jnp.bfloat16
    )
    spread = (in_proj[:, :, None] * member[:, None, :]).reshape(tokens_here, KIN * queries)
    owned_rows = lax.psum_scatter(
        lax.dot_general(
            out_proj, spread, (((0,), (0,)), ((), ())), preferred_element_type=jnp.float32
        ),
        "rows",
        scatter_dimension=0,
        tiled=True,
    )
    owned_block = owned_rows.astype(jnp.bfloat16).reshape(owned_count * KIN, queries)
    block = inverse
    precond_block = jnp.dot(
        block,
        lax.all_gather(owned_block, "rows", axis=0, tiled=True),
        preferred_element_type=jnp.float32,
    ).astype(jnp.bfloat16)
    block = stored_rows
    scores = jnp.dot(
        block,
        lax.all_gather(precond_block, "rows", axis=0, tiled=True),
        preferred_element_type=jnp.float32,
    )
    example_member = (
        example_ids[0][:, None] == jnp.arange(EX_DEV, dtype=jnp.int32)[None, :]
    ).astype(jnp.float32)
    return lax.dot_general(
        example_member,
        scores,
        (((0,), (0,)), ((), ())),
        precision=lax.Precision.HIGHEST,
        preferred_element_type=jnp.float32,
    )


def solution(mesh):
    placed = (
        P(("groups", "rows"), None),
        P(("groups", "rows"), None),
        P(),
        P(),
        P("rows", None),
        P(("groups", "rows"), None),
        P(("groups", "rows")),
        P(("groups", "rows"), None),
    )
    return jax.shard_map(
        on_device,
        mesh=mesh,
        in_specs=placed,
        out_specs=P(("groups", "rows"), None),
        check_vma=False,
    )
```

profile of v0, /device:TPU:0, one launch (start us, length us, event | category | flops | bytes accessed | tf_op | source)
XLA Modules:
  0.0 168.4 jit_solution(15323579211038104771)
XLA Ops:
  6.5 0.0 copy-start
  6.5 0.0 copy-start.1
  6.5 0.0 copy-start.2
  6.5 0.0 reduce-scatter.2.cloned.1.call-start
  6.5 0.9 fusion.6
  7.4 3.2 %convolution_convert_fusion.1 = bf16[16,128]{1,0:T(8,128)(2,1)S(1)} fusion(bf16[16,14336]{1,0:T(8,128)(2,1)} %param.8, bf16[128,14336]{1,0:T(8,128)(2,1)} %param.10), kind=kOutput, calls=%fused_computation.2 | convolution fusion | flops 58722304 | bytes 4132864 | tf_op jit(solution)/shard_map/dot_general | solution.py:19
  10.7 0.4 broadcast_multiply_fusion
  11.0 0.8 mul.20
  11.8 0.0 copy-done.1
  11.8 0.0 copy-done.2
  11.8 1.9 %fusion.1 = f32[128,2048]{1,0:T(8,128)} fusion(bf16[16,2048]{1,0:T(8,128)(2,1)S(1)} %mul.20, bf16[16,4096]{1,0:T(8,128)(2,1)S(1)} %copy-done.2, bf16[128,4096]{1,0:T(8,128)(2,1)S(1)} %copy-done.1), kind=kOutput, calls=%fused_computation.4 | convolution fusion | flops 25167872 | bytes 2293760 | tf_op jit(solution)/shard_map/dot_general | solution.py:30
  13.7 0.0 reduce-scatter.2.cloned.1.call-update
  13.8 60.4 %reduce-scatter.2.cloned.1.call-done = f32[8,2048]{1,0:T(8,128)} async-done(((f32[128,2048]{1,0:T(8,128)}), f32[8,2048]{1,0:T(8,128)}) %reduce-scatter.2.cloned.1.call-update) | async-done | bytes 65552 | tf_op jit(solution)/shard_map/reduce_scatter | solution.py:29
  74.2 0.8 convert_element_type.26
  75.0 0.2 reshape.27
  75.2 49.6 %all_gather.6 = bf16[16384,16]{1,0:T(8,128)(2,1)S(1)} all-gather(bf16[1024,16]{1,0:T(8,128)(2,1)S(1)} %reshape.27), channel_id=1, replica_groups=mesh['groups'=2,'rows'=16] {'rows'}, dimensions={0}, use_global_device_ids=true | all-gather | bytes 557056 | tf_op jit(solution)/shard_map/all_gather | solution.py:41
  124.9 0.0 copy-start.3
  124.9 14.4 %fusion = bf16[1024,16]{0,1:T(8,128)(2,1)S(1)} fusion(bf16[16384,16]{1,0:T(8,128)(2,1)S(1)} %all_gather.6, bf16[1024,16384]{1,0:T(8,128)(2,1)} %param.12), kind=kOutput, calls=%fused_computation.1 | convolution fusion | flops 536887296 | bytes 34111488 | tf_op jit(solution)/shard_map/dot_general | solution.py:39
  139.3 20.9 %all_gather.7 = bf16[16384,16]{0,1:T(8,128)(2,1)S(1)} all-gather(bf16[1024,16]{0,1:T(8,128)(2,1)S(1)} %fusion), channel_id=1, replica_groups=mesh['groups'=2,'rows'=16] {'rows'}, dimensions={0}, use_global_device_ids=true | all-gather | bytes 557056 | tf_op jit(solution)/shard_map/all_gather | solution.py:47
  160.2 0.0 copy-done
  160.2 0.5 fusion.7
  160.7 0.0 copy-done.3
  160.7 0.9 fusion.3
Async XLA Ops:
  6.5 153.6 %copy-start = (bf16[48,16384]{1,0:T(8,128)(2,1)S(1)}, bf16[48,16384]{1,0:T(8,128)(2,1)}, u32[]{:S(2)}) copy-start(bf16[48,16384]{1,0:T(8,128)(2,1)} %param.13) | copy-start | bytes 4718596
  6.5 5.2 %copy-start.1 = (bf16[128,4096]{1,0:T(8,128)(2,1)S(1)}, bf16[128,4096]{1,0:T(8,128)(2,1)}, u32[]{:S(2)}) copy-start(bf16[128,4096]{1,0:T(8,128)(2,1)} %param.11) | copy-start | bytes 3145732
  6.5 5.2 %copy-start.2 = (bf16[16,4096]{1,0:T(8,128)(2,1)S(1)}, bf16[16,4096]{1,0:T(8,128)(2,1)}, u32[]{:S(2)}) copy-start(bf16[16,4096]{1,0:T(8,128)(2,1)} %param.9) | copy-start | bytes 393220
  6.5 67.6 %reduce-scatter.2.cloned.1.call-start = ((), (), s32[]{:S(2)}) async-start(), calls=%async_computation.1 | async-start | bytes 1114112 | tf_op jit(solution)/shard_map/reduce_scatter | solution.py:29
  124.9 35.8 %copy-start.3 = (s32[1,48]{1,0:T(1,128)S(1)}, s32[1,48]{1,0:T(1,128)}, u32[]{:S(2)}) copy-start(s32[1,48]{1,0:T(1,128)} %param.15) | copy-start | bytes 580
Sparse Core Ops, SparseCore 0:
  13.9 60.2 reduce-scatter.1
where the time goes:
time: 169 us; the launch traced here: 168 us
  blocking collectives  70.5 us (42%)
  waiting for transfers between devices  60.4 us (36%)
  matrix products  21 us (12%)
  between operations  13.4 us (8%)
  other arithmetic  2.07 us (1%)
    reduce_scatter x1, waiting for transfers between devices, on_device(): lax.psum_scatter(lax.dot_general(out_proj, spread, (((0,), (0,)), ((), ()...  60.4 us
    all_gather x1, blocking collectives, on_device(): lax.all_gather(owned_block, 'rows', axis=0, tiled=True)  49.6 us
    all_gather x1, blocking collectives, on_device(): lax.all_gather(precond_block, 'rows', axis=0, tiled=True)  20.9 us
    dot_general x1, matrix products, on_device(): jnp.dot(block, lax.all_gather(owned_block, 'rows', axis=0, tiled=True), p...  14.4 us
  transfers between devices with their start and end apart: 1, of which 1 were waited for; matrix products, arithmetic and copies ran while one was open for 0% of the time, Pallas kernels for 0%

commit v1 on v0

v1 whole, which is shorter than its diff:
```python
import functools

import jax
import jax.numpy as jnp
from jax import lax
from jax.experimental import pallas as pl
from jax.experimental.pallas import tpu as pltpu
from jax.sharding import PartitionSpec as P

LANES = 128
QRY_DEV = 1
EX_DEV = 16
NT = (((1,), (1,)), ((), ()))
VMEM = pl.BlockSpec(memory_space=pltpu.VMEM)
ANY = pl.BlockSpec(memory_space=pl.ANY)


def chunk_of(total, most):
    size = most
    while total % size:
        size //= 2
    return size


def round_up(n, m):
    return -(-n // m) * m


def project_kernel(acts, grads, in_w, out_w, ids, tok, acts_v, grads_v, in_v, out_v, sem, *, step):
    pieces = [(grads, grads_v, out_w, out_v, 0, grads.shape[1])]
    pieces += [(acts, acts_v, in_w, in_v, k, step) for k in range(0, acts.shape[1], step)]
    copies = []
    for n, (x, x_v, w, w_v, k, size) in enumerate(pieces):
        cols = pl.ds(k, size)
        copies.append(
            (
                pltpu.make_async_copy(x.at[:, cols], x_v.at[:, cols], sem.at[n, 0]),
                pltpu.make_async_copy(w.at[:, cols], w_v.at[:, cols], sem.at[n, 1]),
            )
        )
    for pair in copies:
        for copy in pair:
            copy.start()
    tokens, kin = acts.shape[0], in_w.shape[0]
    kout, width = out_w.shape[0], tok.shape[1] - in_w.shape[0] - out_w.shape[0]
    row = lax.broadcasted_iota(jnp.int32, (tokens, tokens), 0)
    col = lax.broadcasted_iota(jnp.int32, (tokens, tokens), 1)
    mine = jnp.sum(jnp.where(row == col, ids[...], 0), axis=1, keepdims=True)
    query = lax.broadcasted_iota(jnp.int32, (tokens, width), 1)
    tok[:, kin + kout :] = jnp.where(query == mine, 1.0, 0.0).astype(jnp.bfloat16)
    total = jnp.zeros((tokens, kin), jnp.float32)
    for n, (x, x_v, w, w_v, k, size) in enumerate(pieces):
        for copy in copies[n]:
            copy.wait()
        part = lax.dot_general(
            x_v[:, k : k + size], w_v[:, k : k + size], NT, preferred_element_type=jnp.float32
        )
        if n == 0:
            tok[:, kin : kin + kout] = part.astype(jnp.bfloat16)
        else:
            total += part
    tok[:, :kin] = total.astype(jnp.bfloat16)


def project(acts, grads, in_w, out_w, ids, queries):
    tokens, ff = acts.shape
    step = chunk_of(ff, 2048)
    width = in_w.shape[0] + out_w.shape[0] + round_up(queries, LANES)
    return pl.pallas_call(
        functools.partial(project_kernel, step=step),
        in_specs=[ANY] * 4 + [VMEM],
        out_specs=VMEM,
        out_shape=jax.ShapeDtypeStruct((tokens, width), jnp.bfloat16),
        scratch_shapes=[
            pltpu.VMEM(acts.shape, acts.dtype),
            pltpu.VMEM(grads.shape, grads.dtype),
            pltpu.VMEM(in_w.shape, in_w.dtype),
            pltpu.VMEM(out_w.shape, out_w.dtype),
            pltpu.SemaphoreType.DMA((ff // step + 1, 2)),
        ],
        compiler_params=pltpu.CompilerParams(vmem_limit_bytes=8 << 20),
        name="project",
    )(acts, grads, in_w, out_w, ids)


def precond_kernel(tok, inverse, out, out_t, member_t, acc, *, kin, kout, per, queries):
    out_t[...] = tok[:, kin : kin + kout].astype(jnp.float32).T.astype(jnp.bfloat16)
    member_t[...] = (
        tok[:, kin + kout :].astype(jnp.float32).T[:queries].astype(jnp.bfloat16)
    )
    acc[...] = jnp.zeros_like(acc)

    def step(s):
        o = out_t[pl.ds(pl.multiple_of(s * per, per), per), :]
        weighted = (o[:, None, :] * member_t[...][None, :, :]).reshape(per * queries, o.shape[1])
        g = jnp.dot(weighted, tok[:, :kin], preferred_element_type=jnp.float32)
        g = g.astype(jnp.bfloat16)
        g = jnp.concatenate([g[k * queries : (k + 1) * queries] for k in range(per)], axis=1)
        block = inverse[:, pl.ds(pl.multiple_of(s * per * kin, per * kin), per * kin)]
        acc[...] += lax.dot_general(g, block, NT, preferred_element_type=jnp.float32)

    pl.loop(0, kout // per)(step)
    out[...] = acc[...].astype(jnp.bfloat16)


def precondition(tok, inverse, kin, kout, queries):
    rows, coords = inverse.shape
    tokens = tok.shape[0]
    per = chunk_of(kout, 16)
    return pl.pallas_call(
        functools.partial(precond_kernel, kin=kin, kout=kout, per=per, queries=queries),
        in_specs=[VMEM, VMEM],
        out_specs=VMEM,
        out_shape=jax.ShapeDtypeStruct((queries, rows), jnp.bfloat16),
        scratch_shapes=[
            pltpu.VMEM((kout, tokens), jnp.bfloat16),
            pltpu.VMEM((queries, tokens), jnp.bfloat16),
            pltpu.VMEM((queries, rows), jnp.float32),
        ],
        compiler_params=pltpu.CompilerParams(vmem_limit_bytes=16 << 20),
        cost_estimate=pl.CostEstimate(
            flops=2 * queries * rows * coords,
            bytes_accessed=2 * rows * coords,
            transcendentals=0,
        ),
        name="precondition",
    )(tok, inverse)


def score_kernel(near, far, stored, ids, out, *, masks, axis):
    me = lax.axis_index(axis)
    rows = near.shape[2]
    scores = jnp.zeros((stored.shape[0], near.shape[1]), jnp.float32)
    half = len(masks) // 2
    for n, mask in enumerate(masks):
        block = near[n] if n < half else far[n - half]
        start = pl.multiple_of((me ^ mask) * rows, rows)
        scores += lax.dot_general(
            stored[:, pl.ds(start, rows)], block, NT, preferred_element_type=jnp.float32
        )
    example = lax.broadcasted_iota(jnp.int32, (out.shape[0], ids.shape[1]), 0)
    member = jnp.where(example == ids[...], 1.0, 0.0)
    out[...] = jnp.dot(
        member, scores, precision=lax.Precision.HIGHEST, preferred_element_type=jnp.float32
    )


def score(near, far, stored, ids, masks, queries):
    return pl.pallas_call(
        functools.partial(score_kernel, masks=masks, axis="rows"),
        in_specs=[VMEM] * 4,
        out_specs=VMEM,
        out_shape=jax.ShapeDtypeStruct((EX_DEV, queries), jnp.float32),
        compiler_params=pltpu.CompilerParams(vmem_limit_bytes=8 << 20),
        name="score",
    )(near, far, stored, ids)


def stages_of(n):
    bits = []
    bit = n // 2
    while bit:
        bits.append(bit)
        bit //= 2
    return bits


def swap(x, bit, n):
    return lax.ppermute(x, "rows", [(i, i ^ bit) for i in range(n)])


def on_device(
    in_acts, out_grads, in_projection, out_projection, inverse, stored_rows, query_ids, example_ids
):
    n = lax.axis_size("rows")
    bits = stages_of(n)
    queries = QRY_DEV * n
    kin, kout = in_projection.shape[0], out_projection.shape[0]
    tok = project(
        in_acts, out_grads, in_projection, out_projection, query_ids[None, :], queries
    )
    inverse, tok = lax.optimization_barrier((inverse, tok))
    for bit in bits:
        tok = jnp.concatenate([tok, swap(tok, bit, n)], axis=0)
    near = precondition(tok, inverse, kin, kout, queries)[None]
    masks = [0]
    for bit in bits:
        masks += [m ^ bit for m in masks]
        far = swap(near, bit, n)
        if bit != bits[-1]:
            near = jnp.concatenate([near, far], axis=0)
    return score(near, far, stored_rows, example_ids, masks, queries)


def solution(mesh):
    placed = (
        P(("groups", "rows"), None),
        P(("groups", "rows"), None),
        P(),
        P(),
        P("rows", None),
        P(("groups", "rows"), None),
        P(("groups", "rows")),
        P(("groups", "rows"), None),
    )
    return jax.shard_map(
        on_device,
        mesh=mesh,
        in_specs=placed,
        out_specs=P(("groups", "rows"), None),
        check_vma=False,
    )
```

time: 169 us -> 63.2 us (0.37)
  blocking collectives: 70.5 us -> 0 us
  waiting for transfers between devices: 60.4 us -> 15.8 us
  matrix products: 21 us -> 0 us
  local copies, waits for them, and re-layouts: 0.99 us -> 16.4 us
  Pallas kernels: 0 us -> 15.3 us
  starting transfers between devices: 0.01 us -> 15.2 us
  between operations: 13.4 us -> 0.07 us
  other arithmetic: 2.07 us -> 0.07 us
    all_gather x2 -> x0, blocking collectives: 70.5 us -> none  [the longest x1 49.6 us: on_device(): lax.all_gather(owned_block, 'rows', axis=0, tiled=True)]
    reduce_scatter x1 -> x0, waiting for transfers between devices: 60.4 us -> none  [on_device(): lax.psum_scatter(lax.dot_general(out_proj, spread, (((0,), (0,)), ((), ()...]
    dot_general x5 -> x0, matrix products: 21 us -> none  [the longest x1 14.4 us: on_device(): jnp.dot(block, lax.all_gather(owned_block, 'rows', axis=0, tiled=True), p...]
    unnamed x8 -> x20, local copies, waits for them, and re-layouts: 0.02 us -> 16.4 us
    ppermute x0 -> x8, waiting for transfers between devices: none -> 15.8 us  [swap(): return lax.ppermute(x, 'rows', [(i, i ^ bit) for i in range(n)])]
    pallas_call x0 -> x3, Pallas kernels: none -> 15.3 us  [the longest x1 10.3 us: precondition(): pl.pallas_call(functools.partial(precond_kernel, kin=kin, kout=kout, per=...]
    ppermute x0 -> x8, starting transfers between devices: none -> 15.2 us  [swap(): return lax.ppermute(x, 'rows', [(i, i ^ bit) for i in range(n)])]
    convert_element_type x2 -> x0, other arithmetic: 1.72 us -> none  [the longest x1 0.88 us: on_device(): (query_ids[:, None] == jnp.arange(queries, dtype=jnp.int32)[None, :]).ast...]
  transfers between devices with their start and end apart: 1 -> 8, of which waited for: 1 -> 8; matrix products, arithmetic and copies ran while one was open for 0% -> 0% of each run, Pallas kernels for 0% -> 0%
where the time goes in v1:
time: 63.2 us; the launch traced here: 62.9 us
  local copies, waits for them, and re-layouts  16.4 us (26%)
  waiting for transfers between devices  15.8 us (25%)
  Pallas kernels  15.3 us (24%)
  starting transfers between devices  15.2 us (24%)
    unnamed x20, local copies, waits for them, and re-layouts  16.4 us
    ppermute x8, waiting for transfers between devices, swap(): return lax.ppermute(x, 'rows', [(i, i ^ bit) for i in range(n)])  15.8 us
    ppermute x8, starting transfers between devices, swap(): return lax.ppermute(x, 'rows', [(i, i ^ bit) for i in range(n)])  15.2 us
    pallas_call x1, Pallas kernels, precondition(): pl.pallas_call(functools.partial(precond_kernel, kin=kin, kout=kout, per=...  10.3 us
    pallas_call x1, Pallas kernels, project(): pl.pallas_call(functools.partial(project_kernel, step=step), in_specs=[AN...  3.69 us
    pallas_call x1, Pallas kernels, score(): pl.pallas_call(functools.partial(score_kernel, masks=masks, axis='rows'),...  1.31 us
  transfers between devices with their start and end apart: 8, of which 8 were waited for; matrix products, arithmetic and copies ran while one was open for 0% of the time, Pallas kernels for 0%

profile of v1, /device:TPU:0, one launch (start us, length us, event | category | flops | bytes accessed | tf_op | source)
XLA Modules:
  0.0 62.9 jit_solution(18171062168454554152)
XLA Ops:
  0.0 2.0 %copy-done.1 = bf16[128,14336]{1,0:T(8,128)(2,1)S(1)} copy-done((bf16[128,14336]{1,0:T(8,128)(2,1)S(1)}, bf16[128,14336]{1,0:T(8,128)(2,1)}, u32[]{:S(2)}) %copy-start.1) | copy-done | bytes 3670040
  2.0 1.2 %copy-done.3 = bf16[128,4096]{1,0:T(8,128)(2,1)S(1)} copy-done((bf16[128,4096]{1,0:T(8,128)(2,1)S(1)}, bf16[128,4096]{1,0:T(8,128)(2,1)}, u32[]{:S(2)}) %copy-start.3) | copy-done | bytes 1048600
  3.3 1.0 %copy-done.4 = bf16[16,14336]{1,0:T(8,128)(2,1)S(1)} copy-done((bf16[16,14336]{1,0:T(8,128)(2,1)S(1)}, bf16[16,14336]{1,0:T(8,128)(2,1)}, u32[]{:S(2)}) %copy-start.4) | copy-done | bytes 458776
  4.3 0.9 %copy-done.5 = bf16[16,4096]{1,0:T(8,128)(2,1)S(1)} copy-done((bf16[16,4096]{1,0:T(8,128)(2,1)S(1)}, bf16[16,4096]{1,0:T(8,128)(2,1)}, u32[]{:S(2)}) %copy-start.5) | copy-done | bytes 131096
  5.2 0.7 %copy-done.6 = s32[16]{0:T(128)S(1)} copy-done((s32[16]{0:T(128)S(1)}, s32[16]{0:T(128)}, u32[]{:S(2)}) %copy-start.6) | copy-done | bytes 88
  5.8 3.7 %project.1 = bf16[16,384]{1,0:T(8,128)(2,1)S(1)} custom-call(bf16[16,14336]{1,0:T(8,128)(2,1)S(1)} %copy-done.4, bf16[16,4096]{1,0:T(8,128)(2,1)S(1)} %copy-done.5, bf16[128,14336]{1,0:T(8,128)(2,1)S(1)} %copy-done.1, bf16[128,4096]{1,0:T(8,128)(2,1)S(1)} %copy-done.3, s32[1,16]{1,0:T(1,128)S(1)} %bitcast.6), custom_call_target="tpu_custom_call" | custom-call | tf_op jit(solution)/shard_map/project/pallas_call | solution.py:69
  9.5 4.1 %collective-permute-start = (bf16[16,384]{1,0:T(8,128)(2,1)S(1)}, bf16[16,384]{1,0:T(8,128)(2,1)S(1)}, u32[]{:S(2)}, u32[]{:S(2)}) collective-permute-start(bf16[16,384]{1,0:T(8,128)(2,1)S(1)} %project.1), channel_id=1, source_target_pairs={{0,8},{1,9},{2,10},{3,11},{4,12},{5,13},{6,14},{7,15},{8,0},{9,1},... | collective-permute-start | bytes 36872 | tf_op jit(solution)/shard_map/ppermute | solution.py:169
  13.7 1.7 %collective-permute-done = bf16[16,384]{1,0:T(8,128)(2,1)S(1)} collective-permute-done((bf16[16,384]{1,0:T(8,128)(2,1)S(1)}, bf16[16,384]{1,0:T(8,128)(2,1)S(1)}, u32[]{:S(2)}, u32[]{:S(2)}) %collective-permute-start) | collective-permute-done | bytes 12320 | tf_op jit(solution)/shard_map/ppermute | solution.py:169
  15.4 1.9 %collective-permute-start.1 = (bf16[32,384]{1,0:T(8,128)(2,1)S(1)}, bf16[32,384]{1,0:T(8,128)(2,1)S(1)}, u32[]{:S(2)}, u32[]{:S(2)}) collective-permute-start(bf16[32,384]{1,0:T(8,128)(2,1)S(1)} %pad_maximum_fusion.5), channel_id=1, source_target_pairs={{0,4},{1,5},{2,6},{3,7},{4,0},{5,1},{6,2},{7,3},{8,12},{9,13},{10,... | collective-permute-start | bytes 73736 | tf_op jit(solution)/shard_map/ppermute | solution.py:169
  17.3 1.9 %collective-permute-done.1 = bf16[32,384]{1,0:T(8,128)(2,1)S(1)} collective-permute-done((bf16[32,384]{1,0:T(8,128)(2,1)S(1)}, bf16[32,384]{1,0:T(8,128)(2,1)S(1)}, u32[]{:S(2)}, u32[]{:S(2)}) %collective-permute-start.1) | collective-permute-done | bytes 24608 | tf_op jit(solution)/shard_map/ppermute | solution.py:169
  19.2 1.9 %collective-permute-start.2 = (bf16[64,384]{1,0:T(8,128)(2,1)S(1)}, bf16[64,384]{1,0:T(8,128)(2,1)S(1)}, u32[]{:S(2)}, u32[]{:S(2)}) collective-permute-start(bf16[64,384]{1,0:T(8,128)(2,1)S(1)} %pad_maximum_fusion.4), channel_id=1, source_target_pairs={{0,2},{1,3},{2,0},{3,1},{4,6},{5,7},{6,4},{7,5},{8,10},{9,11},{10,... | collective-permute-start | bytes 147464 | tf_op jit(solution)/shard_map/ppermute | solution.py:169
  21.1 2.2 %collective-permute-done.2 = bf16[64,384]{1,0:T(8,128)(2,1)S(1)} collective-permute-done((bf16[64,384]{1,0:T(8,128)(2,1)S(1)}, bf16[64,384]{1,0:T(8,128)(2,1)S(1)}, u32[]{:S(2)}, u32[]{:S(2)}) %collective-permute-start.2) | collective-permute-done | bytes 49184 | tf_op jit(solution)/shard_map/ppermute | solution.py:169
  23.3 0.1 collective-permute-start.3
  23.4 1.3 %collective-permute-done.3 = bf16[128,384]{1,0:T(8,128)(2,1)S(1)} collective-permute-done((bf16[128,384]{1,0:T(8,128)(2,1)S(1)}, bf16[128,384]{1,0:T(8,128)(2,1)S(1)}, u32[]{:S(2)}, u32[]{:S(2)}) %collective-permute-start.3) | collective-permute-done | bytes 98336 | tf_op jit(solution)/shard_map/ppermute | solution.py:169
  24.7 10.5 %copy-done = bf16[1024,16384]{1,0:T(8,128)(2,1)S(1)} copy-done((bf16[1024,16384]{1,0:T(8,128)(2,1)S(1)}, bf16[1024,16384]{1,0:T(8,128)(2,1)}, u32[]{:S(2)}) %copy-start) | copy-done | bytes 33554456
  35.2 10.3 %precondition.1 = bf16[16,1024]{1,0:T(8,128)(2,1)S(1)} custom-call(bf16[256,384]{1,0:T(8,128)(2,1)S(1)} %constant_dynamic-update-slice_fusion.tok, bf16[1024,16384]{1,0:T(8,128)(2,1)S(1)} %copy-done), custom_call_target="tpu_custom_call" | custom-call | flops 536870912 | bytes 33554432 | tf_op jit(solution)/shard_map/precondition/pallas_call | solution.py:110
  45.5 2.9 %collective-permute-start.4 = (bf16[1,16,1024]{2,1,0:T(8,128)(2,1)S(1)}, bf16[1,16,1024]{2,1,0:T(8,128)(2,1)S(1)}, u32[]{:S(2)}, u32[]{:S(2)}) collective-permute-start(bf16[1,16,1024]{2,1,0:T(8,128)(2,1)S(1)} %bitcast.2), channel_id=1, source_target_pairs={{0,8},{1,9},{2,10},{3,11},{4,12},{5,13},{6,14},{7,15},{8,0},{9,1},... | collective-permute-start | bytes 98312 | tf_op jit(solution)/shard_map/ppermute | solution.py:169
  48.4 1.9 %collective-permute-done.4 = bf16[1,16,1024]{2,1,0:T(8,128)(2,1)S(1)} collective-permute-done((bf16[1,16,1024]{2,1,0:T(8,128)(2,1)S(1)}, bf16[1,16,1024]{2,1,0:T(8,128)(2,1)S(1)}, u32[]{:S(2)}, u32[]{:S(2)}) %collective-permute-start.4) | collective-permute-done | bytes 32800 | tf_op jit(solution)/shard_map/ppermute | solution.py:169
  50.3 2.0 %collective-permute-start.5 = (bf16[2,16,1024]{2,1,0:T(8,128)(2,1)S(1)}, bf16[2,16,1024]{2,1,0:T(8,128)(2,1)S(1)}, u32[]{:S(2)}, u32[]{:S(2)}) collective-permute-start(bf16[2,16,1024]{2,1,0:T(8,128)(2,1)S(1)} %pad_maximum_fusion.3), channel_id=1, source_target_pairs={{0,4},{1,5},{2,6},{3,7},{4,0},{5,1},{6,2},{7,3},{8,12},{9,13},{10,... | collective-permute-start | bytes 196616 | tf_op jit(solution)/shard_map/ppermute | solution.py:169
  52.3 2.4 %collective-permute-done.5 = bf16[2,16,1024]{2,1,0:T(8,128)(2,1)S(1)} collective-permute-done((bf16[2,16,1024]{2,1,0:T(8,128)(2,1)S(1)}, bf16[2,16,1024]{2,1,0:T(8,128)(2,1)S(1)}, u32[]{:S(2)}, u32[]{:S(2)}) %collective-permute-start.5) | collective-permute-done | bytes 65568 | tf_op jit(solution)/shard_map/ppermute | solution.py:169
  54.7 2.3 %collective-permute-start.6 = (bf16[4,16,1024]{2,1,0:T(8,128)(2,1)S(1)}, bf16[4,16,1024]{2,1,0:T(8,128)(2,1)S(1)}, u32[]{:S(2)}, u32[]{:S(2)}) collective-permute-start(bf16[4,16,1024]{2,1,0:T(8,128)(2,1)S(1)} %pad_maximum_fusion.1), channel_id=1, source_target_pairs={{0,2},{1,3},{2,0},{3,1},{4,6},{5,7},{6,4},{7,5},{8,10},{9,11},{10,... | collective-permute-start | bytes 393224 | tf_op jit(solution)/shard_map/ppermute | solution.py:169
  57.0 2.9 %collective-permute-done.6 = bf16[4,16,1024]{2,1,0:T(8,128)(2,1)S(1)} collective-permute-done((bf16[4,16,1024]{2,1,0:T(8,128)(2,1)S(1)}, bf16[4,16,1024]{2,1,0:T(8,128)(2,1)S(1)}, u32[]{:S(2)}, u32[]{:S(2)}) %collective-permute-start.6) | collective-permute-done | bytes 131104 | tf_op jit(solution)/shard_map/ppermute | solution.py:169
  60.0 1.5 %collective-permute-done.7.far = bf16[8,16,1024]{2,1,0:T(8,128)(2,1)S(1)} collective-permute-done((bf16[8,16,1024]{2,1,0:T(8,128)(2,1)S(1)}, bf16[8,16,1024]{2,1,0:T(8,128)(2,1)S(1)}, u32[]{:S(2)}, u32[]{:S(2)}) %collective-permute-start.7) | collective-permute-done | bytes 262176 | tf_op jit(solution)/shard_map/ppermute | solution.py:169
  61.6 1.3 %score.1 = f32[16,16]{1,0:T(8,128)} custom-call(bf16[8,16,1024]{2,1,0:T(8,128)(2,1)S(1)} %pad_maximum_fusion.near, bf16[8,16,1024]{2,1,0:T(8,128)(2,1)S(1)} %collective-permute-done.7.far, bf16[48,16384]{1,0:T(8,128)(2,1)S(1)} %copy-done.2, s32[1,48]{1,0:T(1,128)S(1)} %copy-done.7), custom_call_target="tpu_custom_call" | custom-call | tf_op jit(solution)/shard_map/score/pallas_call | solution.py:149
  (22 shorter events, 0.2 us)
Async XLA Ops:
  0.0 2.0 %copy-start.1 = (bf16[128,14336]{1,0:T(8,128)(2,1)S(1)}, bf16[128,14336]{1,0:T(8,128)(2,1)}, u32[]{:S(2)}) copy-start(bf16[128,14336]{1,0:T(8,128)(2,1)} %in_w.1) | copy-start | bytes 11010052
  2.0 1.2 %copy-start.3 = (bf16[128,4096]{1,0:T(8,128)(2,1)S(1)}, bf16[128,4096]{1,0:T(8,128)(2,1)}, u32[]{:S(2)}) copy-start(bf16[128,4096]{1,0:T(8,128)(2,1)} %out_w.1) | copy-start | bytes 3145732
  3.3 1.0 %copy-start.4 = (bf16[16,14336]{1,0:T(8,128)(2,1)S(1)}, bf16[16,14336]{1,0:T(8,128)(2,1)}, u32[]{:S(2)}) copy-start(bf16[16,14336]{1,0:T(8,128)(2,1)} %acts.1) | copy-start | bytes 1376260
  4.3 0.9 %copy-start.5 = (bf16[16,4096]{1,0:T(8,128)(2,1)S(1)}, bf16[16,4096]{1,0:T(8,128)(2,1)}, u32[]{:S(2)}) copy-start(bf16[16,4096]{1,0:T(8,128)(2,1)} %grads.1) | copy-start | bytes 393220
  5.2 0.7 %copy-start.6 = (s32[16]{0:T(128)S(1)}, s32[16]{0:T(128)}, u32[]{:S(2)}) copy-start(s32[16]{0:T(128)} %param.14) | copy-start | bytes 196
  9.5 5.8 %collective-permute-start = (bf16[16,384]{1,0:T(8,128)(2,1)S(1)}, bf16[16,384]{1,0:T(8,128)(2,1)S(1)}, u32[]{:S(2)}, u32[]{:S(2)}) collective-permute-start(bf16[16,384]{1,0:T(8,128)(2,1)S(1)} %project.1), channel_id=1, source_target_pairs={{0,8},{1,9},{2,10},{3,11},{4,12},{5,13},{6,14},{7,15},{8,0},{9,1},... | collective-permute-start | bytes 36872 | tf_op jit(solution)/shard_map/ppermute | solution.py:169
  15.4 3.8 %collective-permute-start.1 = (bf16[32,384]{1,0:T(8,128)(2,1)S(1)}, bf16[32,384]{1,0:T(8,128)(2,1)S(1)}, u32[]{:S(2)}, u32[]{:S(2)}) collective-permute-start(bf16[32,384]{1,0:T(8,128)(2,1)S(1)} %pad_maximum_fusion.5), channel_id=1, source_target_pairs={{0,4},{1,5},{2,6},{3,7},{4,0},{5,1},{6,2},{7,3},{8,12},{9,13},{10,... | collective-permute-start | bytes 73736 | tf_op jit(solution)/shard_map/ppermute | solution.py:169
  19.2 4.1 %collective-permute-start.2 = (bf16[64,384]{1,0:T(8,128)(2,1)S(1)}, bf16[64,384]{1,0:T(8,128)(2,1)S(1)}, u32[]{:S(2)}, u32[]{:S(2)}) collective-permute-start(bf16[64,384]{1,0:T(8,128)(2,1)S(1)} %pad_maximum_fusion.4), channel_id=1, source_target_pairs={{0,2},{1,3},{2,0},{3,1},{4,6},{5,7},{6,4},{7,5},{8,10},{9,11},{10,... | collective-permute-start | bytes 147464 | tf_op jit(solution)/shard_map/ppermute | solution.py:169
  23.3 1.4 %collective-permute-start.3 = (bf16[128,384]{1,0:T(8,128)(2,1)S(1)}, bf16[128,384]{1,0:T(8,128)(2,1)S(1)}, u32[]{:S(2)}, u32[]{:S(2)}) collective-permute-start(bf16[128,384]{1,0:T(8,128)(2,1)S(1)} %pad_maximum_fusion.2), channel_id=1, source_target_pairs={{0,1},{1,0},{2,3},{3,2},{4,5},{5,4},{6,7},{7,6},{8,9},{9,8},{10,11... | collective-permute-start | bytes 294920 | tf_op jit(solution)/shard_map/ppermute | solution.py:169
  24.7 10.5 %copy-start = (bf16[1024,16384]{1,0:T(8,128)(2,1)S(1)}, bf16[1024,16384]{1,0:T(8,128)(2,1)}, u32[]{:S(2)}) copy-start(bf16[1024,16384]{1,0:T(8,128)(2,1)} %inverse) | copy-start | bytes 100663296
  35.2 26.3 %copy-start.2 = (bf16[48,16384]{1,0:T(8,128)(2,1)S(1)}, bf16[48,16384]{1,0:T(8,128)(2,1)}, u32[]{:S(2)}) copy-start(bf16[48,16384]{1,0:T(8,128)(2,1)} %stored.1) | copy-start | bytes 4718596
  35.2 26.3 %copy-start.7 = (s32[1,48]{1,0:T(1,128)S(1)}, s32[1,48]{1,0:T(1,128)}, u32[]{:S(2)}) copy-start(s32[1,48]{1,0:T(1,128)} %ids.1) | copy-start | bytes 580
  45.5 4.8 %collective-permute-start.4 = (bf16[1,16,1024]{2,1,0:T(8,128)(2,1)S(1)}, bf16[1,16,1024]{2,1,0:T(8,128)(2,1)S(1)}, u32[]{:S(2)}, u32[]{:S(2)}) collective-permute-start(bf16[1,16,1024]{2,1,0:T(8,128)(2,1)S(1)} %bitcast.2), channel_id=1, source_target_pairs={{0,8},{1,9},{2,10},{3,11},{4,12},{5,13},{6,14},{7,15},{8,0},{9,1},... | collective-permute-start | bytes 98312 | tf_op jit(solution)/shard_map/ppermute | solution.py:169
  50.3 4.3 %collective-permute-start.5 = (bf16[2,16,1024]{2,1,0:T(8,128)(2,1)S(1)}, bf16[2,16,1024]{2,1,0:T(8,128)(2,1)S(1)}, u32[]{:S(2)}, u32[]{:S(2)}) collective-permute-start(bf16[2,16,1024]{2,1,0:T(8,128)(2,1)S(1)} %pad_maximum_fusion.3), channel_id=1, source_target_pairs={{0,4},{1,5},{2,6},{3,7},{4,0},{5,1},{6,2},{7,3},{8,12},{9,13},{10,... | collective-permute-start | bytes 196616 | tf_op jit(solution)/shard_map/ppermute | solution.py:169
  54.7 5.2 %collective-permute-start.6 = (bf16[4,16,1024]{2,1,0:T(8,128)(2,1)S(1)}, bf16[4,16,1024]{2,1,0:T(8,128)(2,1)S(1)}, u32[]{:S(2)}, u32[]{:S(2)}) collective-permute-start(bf16[4,16,1024]{2,1,0:T(8,128)(2,1)S(1)} %pad_maximum_fusion.1), channel_id=1, source_target_pairs={{0,2},{1,3},{2,0},{3,1},{4,6},{5,7},{6,4},{7,5},{8,10},{9,11},{10,... | collective-permute-start | bytes 393224 | tf_op jit(solution)/shard_map/ppermute | solution.py:169
  60.0 1.6 %collective-permute-start.7 = (bf16[8,16,1024]{2,1,0:T(8,128)(2,1)S(1)}, bf16[8,16,1024]{2,1,0:T(8,128)(2,1)S(1)}, u32[]{:S(2)}, u32[]{:S(2)}) collective-permute-start(bf16[8,16,1024]{2,1,0:T(8,128)(2,1)S(1)} %pad_maximum_fusion.near), channel_id=1, source_target_pairs={{0,1},{1,0},{2,3},{3,2},{4,5},{5,4},{6,7},{7,6},{8,9},{9,8},{10,11... | collective-permute-start | bytes 786440 | tf_op jit(solution)/shard_map/ppermute | solution.py:169

commit v2 on v1

--- a/solution.py
+++ b/solution.py
@@ -13,6 +13,7 @@
 NT = (((1,), (1,)), ((), ()))
 VMEM = pl.BlockSpec(memory_space=pltpu.VMEM)
 ANY = pl.BlockSpec(memory_space=pl.ANY)
+VMEM_BYTES = 67_043_328 - (1 << 16)
 
 
 def chunk_of(total, most):
@@ -26,7 +27,7 @@
     return -(-n // m) * m
 
 
-def project_kernel(acts, grads, in_w, out_w, ids, tok, acts_v, grads_v, in_v, out_v, sem, *, step):
+def project_kernel(acts, grads, in_w, out_w, raw, acts_v, grads_v, in_v, out_v, sem, *, step):
     pieces = [(grads, grads_v, out_w, out_v, 0, grads.shape[1])]
     pieces += [(acts, acts_v, in_w, in_v, k, step) for k in range(0, acts.shape[1], step)]
     copies = []
@@ -41,14 +42,8 @@
     for pair in copies:
         for copy in pair:
             copy.start()
-    tokens, kin = acts.shape[0], in_w.shape[0]
-    kout, width = out_w.shape[0], tok.shape[1] - in_w.shape[0] - out_w.shape[0]
-    row = lax.broadcasted_iota(jnp.int32, (tokens, tokens), 0)
-    col = lax.broadcasted_iota(jnp.int32, (tokens, tokens), 1)
-    mine = jnp.sum(jnp.where(row == col, ids[...], 0), axis=1, keepdims=True)
-    query = lax.broadcasted_iota(jnp.int32, (tokens, width), 1)
-    tok[:, kin + kout :] = jnp.where(query == mine, 1.0, 0.0).astype(jnp.bfloat16)
-    total = jnp.zeros((tokens, kin), jnp.float32)
+    kin = in_w.shape[0]
+    total = None
     for n, (x, x_v, w, w_v, k, size) in enumerate(pieces):
         for copy in copies[n]:
             copy.wait()
@@ -56,19 +51,29 @@
             x_v[:, k : k + size], w_v[:, k : k + size], NT, preferred_element_type=jnp.float32
         )
         if n == 0:
-            tok[:, kin : kin + kout] = part.astype(jnp.bfloat16)
+            raw[:, kin:] = part.astype(jnp.bfloat16)
         else:
-            total += part
-    tok[:, :kin] = total.astype(jnp.bfloat16)
+            total = part if total is None else total + part
+    raw[:, :kin] = total.astype(jnp.bfloat16)
+
+
+def mark_kernel(raw, ids, tok):
+    tokens, done = raw.shape
+    row = lax.broadcasted_iota(jnp.int32, (tokens, tokens), 0)
+    col = lax.broadcasted_iota(jnp.int32, (tokens, tokens), 1)
+    mine = jnp.sum(jnp.where(row == col, ids[...], 0), axis=1, keepdims=True)
+    query = lax.broadcasted_iota(jnp.int32, (tokens, tok.shape[1] - done), 1)
+    tok[:, :done] = raw[...]
+    tok[:, done:] = jnp.where(query == mine, 1.0, 0.0).astype(jnp.bfloat16)
 
 
 def project(acts, grads, in_w, out_w, ids, queries):
     tokens, ff = acts.shape
     step = chunk_of(ff, 2048)
-    width = in_w.shape[0] + out_w.shape[0] + round_up(queries, LANES)
-    return pl.pallas_call(
+    width = in_w.shape[0] + out_w.shape[0]
+    raw = pl.pallas_call(
         functools.partial(project_kernel, step=step),
-        in_specs=[ANY] * 4 + [VMEM],
+        in_specs=[ANY] * 4,
         out_specs=VMEM,
         out_shape=jax.ShapeDtypeStruct((tokens, width), jnp.bfloat16),
         scratch_shapes=[
@@ -78,9 +83,22 @@
             pltpu.VMEM(out_w.shape, out_w.dtype),
             pltpu.SemaphoreType.DMA((ff // step + 1, 2)),
         ],
-        compiler_params=pltpu.CompilerParams(vmem_limit_bytes=8 << 20),
+        compiler_params=pltpu.CompilerParams(vmem_limit_bytes=VMEM_BYTES),
         name="project",
-    )(acts, grads, in_w, out_w, ids)
+    )(acts, grads, in_w, out_w)
+    return pl.pallas_call(
+        mark_kernel,
+        in_specs=[VMEM, VMEM],
+        out_specs=VMEM,
+        out_shape=jax.ShapeDtypeStruct(
+            (tokens, width + round_up(queries, LANES)), jnp.bfloat16
+        ),
+        compiler_params=pltpu.CompilerParams(vmem_limit_bytes=2 << 20),
+        cost_estimate=pl.CostEstimate(
+            flops=10**11, bytes_accessed=10**8, transcendentals=0
+        ),
+        name="mark",
+    )(raw, ids)
 
 
 def precond_kernel(tok, inverse, out, out_t, member_t, acc, *, kin, kout, per, queries):
@@ -179,7 +197,6 @@
     tok = project(
         in_acts, out_grads, in_projection, out_projection, query_ids[None, :], queries
     )
-    inverse, tok = lax.optimization_barrier((inverse, tok))
     for bit in bits:
         tok = jnp.concatenate([tok, swap(tok, bit, n)], axis=0)
     near = precondition(tok, inverse, kin, kout, queries)[None]

time: 63.2 us -> 48.8 us (0.77)
  local copies, waits for them, and re-layouts: 16.4 us -> 0.94 us
  Pallas kernels: 15.3 us -> 16.4 us
    unnamed x20 -> x28, local copies, waits for them, and re-layouts: 16.4 us -> 0.93 us
    pallas_call x1, Pallas kernels: 3.69 us -> 4.76 us  [project(): pl.pallas_call(functools.partial(project_kernel, step=step), in_specs=[AN...]
where the time goes in v2:
time: 48.8 us; the launch traced here: 48.6 us
  Pallas kernels  16.4 us (34%)
  waiting for transfers between devices  15.8 us (32%)
  starting transfers between devices  15.2 us (31%)
  local copies, waits for them, and re-layouts  0.94 us (2%)
    ppermute x8, waiting for transfers between devices, swap(): return lax.ppermute(x, 'rows', [(i, i ^ bit) for i in range(n)])  15.8 us
    ppermute x8, starting transfers between devices, swap(): return lax.ppermute(x, 'rows', [(i, i ^ bit) for i in range(n)])  15.2 us
    pallas_call x1, Pallas kernels, precondition(): pl.pallas_call(functools.partial(precond_kernel, kin=kin, kout=kout, per=...  10.3 us
    pallas_call x1, Pallas kernels, project(): pl.pallas_call(functools.partial(project_kernel, step=step), in_specs=[AN...  4.76 us
    pallas_call x1, Pallas kernels, score(): pl.pallas_call(functools.partial(score_kernel, masks=masks, axis='rows'),...  1.31 us
  transfers between devices with their start and end apart: 8, of which 8 were waited for; matrix products, arithmetic and copies ran while one was open for 0% of the time, Pallas kernels for 0%

profile of v2, /device:TPU:0, one launch (start us, length us, event | category | flops | bytes accessed | tf_op | source)
XLA Modules:
  0.0 48.6 jit_solution(10709887283274720661)
XLA Ops:
  0.0 4.8 %project.1.raw = bf16[16,256]{1,0:T(8,128)(2,1)} custom-call(bf16[16,14336]{1,0:T(8,128)(2,1)} %acts.1, bf16[16,4096]{1,0:T(8,128)(2,1)} %grads.1, bf16[128,14336]{1,0:T(8,128)(2,1)} %in_w.1, bf16[128,4096]{1,0:T(8,128)(2,1)} %out_w.1), custom_call_target="tpu_custom_call" | custom-call | tf_op jit(solution)/shard_map/project/pallas_call | solution.py:74
  4.8 0.0 slice-start
  4.8 0.0 copy-start.1
  4.8 0.8 %copy-done.1 = bf16[16,256]{1,0:T(8,128)(2,1)S(1)} copy-done((bf16[16,256]{1,0:T(8,128)(2,1)S(1)}, bf16[16,256]{1,0:T(8,128)(2,1)}, u32[]{:S(2)}) %copy-start.1) | copy-done | bytes 8216
  5.7 0.1 mark.1
  5.8 4.1 %collective-permute-start = (bf16[16,384]{1,0:T(8,128)(2,1)S(1)}, bf16[16,384]{1,0:T(8,128)(2,1)S(1)}, u32[]{:S(2)}, u32[]{:S(2)}) collective-permute-start(bf16[16,384]{1,0:T(8,128)(2,1)S(1)} %mark.1), channel_id=1, source_target_pairs={{0,8},{1,9},{2,10},{3,11},{4,12},{5,13},{6,14},{7,15},{8,0},{9,1},... | collective-permute-start | bytes 36872 | tf_op jit(solution)/shard_map/ppermute | solution.py:187
  9.8 1.7 %collective-permute-done = bf16[16,384]{1,0:T(8,128)(2,1)S(1)} collective-permute-done((bf16[16,384]{1,0:T(8,128)(2,1)S(1)}, bf16[16,384]{1,0:T(8,128)(2,1)S(1)}, u32[]{:S(2)}, u32[]{:S(2)}) %collective-permute-start) | collective-permute-done | bytes 12320 | tf_op jit(solution)/shard_map/ppermute | solution.py:187
  11.5 1.9 %collective-permute-start.1 = (bf16[32,384]{1,0:T(8,128)(2,1)S(1)}, bf16[32,384]{1,0:T(8,128)(2,1)S(1)}, u32[]{:S(2)}, u32[]{:S(2)}) collective-permute-start(bf16[32,384]{1,0:T(8,128)(2,1)S(1)} %pad_maximum_fusion.5), channel_id=1, source_target_pairs={{0,4},{1,5},{2,6},{3,7},{4,0},{5,1},{6,2},{7,3},{8,12},{9,13},{10,... | collective-permute-start | bytes 73736 | tf_op jit(solution)/shard_map/ppermute | solution.py:187
  13.4 1.9 %collective-permute-done.1 = bf16[32,384]{1,0:T(8,128)(2,1)S(1)} collective-permute-done((bf16[32,384]{1,0:T(8,128)(2,1)S(1)}, bf16[32,384]{1,0:T(8,128)(2,1)S(1)}, u32[]{:S(2)}, u32[]{:S(2)}) %collective-permute-start.1) | collective-permute-done | bytes 24608 | tf_op jit(solution)/shard_map/ppermute | solution.py:187
  15.4 1.9 %collective-permute-start.2 = (bf16[64,384]{1,0:T(8,128)(2,1)S(1)}, bf16[64,384]{1,0:T(8,128)(2,1)S(1)}, u32[]{:S(2)}, u32[]{:S(2)}) collective-permute-start(bf16[64,384]{1,0:T(8,128)(2,1)S(1)} %pad_maximum_fusion.4), channel_id=1, source_target_pairs={{0,2},{1,3},{2,0},{3,1},{4,6},{5,7},{6,4},{7,5},{8,10},{9,11},{10,... | collective-permute-start | bytes 147464 | tf_op jit(solution)/shard_map/ppermute | solution.py:187
  17.2 2.2 %collective-permute-done.2 = bf16[64,384]{1,0:T(8,128)(2,1)S(1)} collective-permute-done((bf16[64,384]{1,0:T(8,128)(2,1)S(1)}, bf16[64,384]{1,0:T(8,128)(2,1)S(1)}, u32[]{:S(2)}, u32[]{:S(2)}) %collective-permute-start.2) | collective-permute-done | bytes 49184 | tf_op jit(solution)/shard_map/ppermute | solution.py:187
  19.5 0.1 collective-permute-start.3
  19.6 1.3 %collective-permute-done.3 = bf16[128,384]{1,0:T(8,128)(2,1)S(1)} collective-permute-done((bf16[128,384]{1,0:T(8,128)(2,1)S(1)}, bf16[128,384]{1,0:T(8,128)(2,1)S(1)}, u32[]{:S(2)}, u32[]{:S(2)}) %collective-permute-start.3) | collective-permute-done | bytes 98336 | tf_op jit(solution)/shard_map/ppermute | solution.py:187
  20.9 0.0 copy-start
  21.0 10.3 %precondition.1 = bf16[16,1024]{1,0:T(8,128)(2,1)S(1)} custom-call(bf16[256,384]{1,0:T(8,128)(2,1)S(1)} %constant_dynamic-update-slice_fusion.tok, bf16[1024,16384]{1,0:T(8,128)(2,1)S(1)} %bitcast.3), custom_call_target="tpu_custom_call" | custom-call | flops 536870912 | bytes 33554432 | tf_op jit(solution)/shard_map/precondition/pallas_call | solution.py:128
  31.2 2.9 %collective-permute-start.4 = (bf16[1,16,1024]{2,1,0:T(8,128)(2,1)S(1)}, bf16[1,16,1024]{2,1,0:T(8,128)(2,1)S(1)}, u32[]{:S(2)}, u32[]{:S(2)}) collective-permute-start(bf16[1,16,1024]{2,1,0:T(8,128)(2,1)S(1)} %bitcast.4), channel_id=1, source_target_pairs={{0,8},{1,9},{2,10},{3,11},{4,12},{5,13},{6,14},{7,15},{8,0},{9,1},... | collective-permute-start | bytes 98312 | tf_op jit(solution)/shard_map/ppermute | solution.py:187
  34.2 1.9 %collective-permute-done.4 = bf16[1,16,1024]{2,1,0:T(8,128)(2,1)S(1)} collective-permute-done((bf16[1,16,1024]{2,1,0:T(8,128)(2,1)S(1)}, bf16[1,16,1024]{2,1,0:T(8,128)(2,1)S(1)}, u32[]{:S(2)}, u32[]{:S(2)}) %collective-permute-start.4) | collective-permute-done | bytes 32800 | tf_op jit(solution)/shard_map/ppermute | solution.py:187
  36.1 2.0 %collective-permute-start.5 = (bf16[2,16,1024]{2,1,0:T(8,128)(2,1)S(1)}, bf16[2,16,1024]{2,1,0:T(8,128)(2,1)S(1)}, u32[]{:S(2)}, u32[]{:S(2)}) collective-permute-start(bf16[2,16,1024]{2,1,0:T(8,128)(2,1)S(1)} %pad_maximum_fusion.3), channel_id=1, source_target_pairs={{0,4},{1,5},{2,6},{3,7},{4,0},{5,1},{6,2},{7,3},{8,12},{9,13},{10,... | collective-permute-start | bytes 196616 | tf_op jit(solution)/shard_map/ppermute | solution.py:187
  38.1 2.4 %collective-permute-done.5 = bf16[2,16,1024]{2,1,0:T(8,128)(2,1)S(1)} collective-permute-done((bf16[2,16,1024]{2,1,0:T(8,128)(2,1)S(1)}, bf16[2,16,1024]{2,1,0:T(8,128)(2,1)S(1)}, u32[]{:S(2)}, u32[]{:S(2)}) %collective-permute-start.5) | collective-permute-done | bytes 65568 | tf_op jit(solution)/shard_map/ppermute | solution.py:187
  40.4 2.3 %collective-permute-start.6 = (bf16[4,16,1024]{2,1,0:T(8,128)(2,1)S(1)}, bf16[4,16,1024]{2,1,0:T(8,128)(2,1)S(1)}, u32[]{:S(2)}, u32[]{:S(2)}) collective-permute-start(bf16[4,16,1024]{2,1,0:T(8,128)(2,1)S(1)} %pad_maximum_fusion.1), channel_id=1, source_target_pairs={{0,2},{1,3},{2,0},{3,1},{4,6},{5,7},{6,4},{7,5},{8,10},{9,11},{10,... | collective-permute-start | bytes 393224 | tf_op jit(solution)/shard_map/ppermute | solution.py:187
  42.7 2.9 %collective-permute-done.6 = bf16[4,16,1024]{2,1,0:T(8,128)(2,1)S(1)} collective-permute-done((bf16[4,16,1024]{2,1,0:T(8,128)(2,1)S(1)}, bf16[4,16,1024]{2,1,0:T(8,128)(2,1)S(1)}, u32[]{:S(2)}, u32[]{:S(2)}) %collective-permute-start.6) | collective-permute-done | bytes 131104 | tf_op jit(solution)/shard_map/ppermute | solution.py:187
  45.7 0.1 collective-permute-start.7
  45.8 1.5 %collective-permute-done.7.far = bf16[8,16,1024]{2,1,0:T(8,128)(2,1)S(1)} collective-permute-done((bf16[8,16,1024]{2,1,0:T(8,128)(2,1)S(1)}, bf16[8,16,1024]{2,1,0:T(8,128)(2,1)S(1)}, u32[]{:S(2)}, u32[]{:S(2)}) %collective-permute-start.7) | collective-permute-done | bytes 262176 | tf_op jit(solution)/shard_map/ppermute | solution.py:187
  47.3 1.3 %score.1 = f32[16,16]{1,0:T(8,128)} custom-call(bf16[8,16,1024]{2,1,0:T(8,128)(2,1)S(1)} %pad_maximum_fusion.near, bf16[8,16,1024]{2,1,0:T(8,128)(2,1)S(1)} %collective-permute-done.7.far, bf16[48,16384]{1,0:T(8,128)(2,1)S(1)} %copy-done, s32[1,48]{1,0:T(1,128)S(1)} %copy-done.2), custom_call_target="tpu_custom_call" | custom-call | tf_op jit(solution)/shard_map/score/pallas_call | solution.py:167
  (32 shorter events, 0.2 us)
Async XLA Ops:
  0.0 4.8 %copy-start.3 = (s32[16]{0:T(128)S(1)}, s32[16]{0:T(128)}, u32[]{:S(2)}) copy-start(s32[16]{0:T(128)} %param.14) | copy-start | bytes 196
  4.8 16.1 %slice-start = ((s8[33554432]{0:T(1024)(128)(4,1)}), s8[4194304]{0:T(1024)(128)(4,1)S(1)}, s32[]{:S(2)}) async-start(s8[33554432]{0:T(1024)(128)(4,1)} %bitcast.2), calls=%async_computation | async-start | bytes 8388608
  4.8 0.8 %copy-start.1 = (bf16[16,256]{1,0:T(8,128)(2,1)S(1)}, bf16[16,256]{1,0:T(8,128)(2,1)}, u32[]{:S(2)}) copy-start(bf16[16,256]{1,0:T(8,128)(2,1)} %project.1.raw) | copy-start | bytes 24580
  5.6 15.2 %slice-start.1 = ((s8[33554432]{0:T(1024)(128)(4,1)}), s8[4194304]{0:T(1024)(128)(4,1)S(1)}, s32[]{:S(2)}) async-start(s8[33554432]{0:T(1024)(128)(4,1)} %bitcast.2), calls=%async_computation.1 | async-start | bytes 8388608
  5.6 15.2 %slice-start.2 = ((s8[33554432]{0:T(1024)(128)(4,1)}), s8[4194304]{0:T(1024)(128)(4,1)S(1)}, s32[]{:S(2)}) async-start(s8[33554432]{0:T(1024)(128)(4,1)} %bitcast.2), calls=%async_computation.2 | async-start | bytes 8388608
  5.6 15.2 %slice-start.3 = ((s8[33554432]{0:T(1024)(128)(4,1)}), s8[4194304]{0:T(1024)(128)(4,1)S(1)}, s32[]{:S(2)}) async-start(s8[33554432]{0:T(1024)(128)(4,1)} %bitcast.2), calls=%async_computation.3 | async-start | bytes 8388608
  5.7 15.2 %slice-start.4 = ((s8[33554432]{0:T(1024)(128)(4,1)}), s8[4194304]{0:T(1024)(128)(4,1)S(1)}, s32[]{:S(2)}) async-start(s8[33554432]{0:T(1024)(128)(4,1)} %bitcast.2), calls=%async_computation.4 | async-start | bytes 8388608
  5.7 15.2 %slice-start.5 = ((s8[33554432]{0:T(1024)(128)(4,1)}), s8[4194304]{0:T(1024)(128)(4,1)S(1)}, s32[]{:S(2)}) async-start(s8[33554432]{0:T(1024)(128)(4,1)} %bitcast.2), calls=%async_computation.5 | async-start | bytes 8388608
  5.7 15.2 %slice-start.6 = ((s8[33554432]{0:T(1024)(128)(4,1)}), s8[4194304]{0:T(1024)(128)(4,1)S(1)}, s32[]{:S(2)}) async-start(s8[33554432]{0:T(1024)(128)(4,1)} %bitcast.2), calls=%async_computation.6 | async-start | bytes 8388608
  5.7 15.2 %slice-start.7 = ((s8[33554432]{0:T(1024)(128)(4,1)}), s8[4194304]{0:T(1024)(128)(4,1)S(1)}, s32[]{:S(2)}) async-start(s8[33554432]{0:T(1024)(128)(4,1)} %bitcast.2), calls=%async_computation.7 | async-start | bytes 8388608
  5.8 5.7 %collective-permute-start = (bf16[16,384]{1,0:T(8,128)(2,1)S(1)}, bf16[16,384]{1,0:T(8,128)(2,1)S(1)}, u32[]{:S(2)}, u32[]{:S(2)}) collective-permute-start(bf16[16,384]{1,0:T(8,128)(2,1)S(1)} %mark.1), channel_id=1, source_target_pairs={{0,8},{1,9},{2,10},{3,11},{4,12},{5,13},{6,14},{7,15},{8,0},{9,1},... | collective-permute-start | bytes 36872 | tf_op jit(solution)/shard_map/ppermute | solution.py:187
  11.5 3.8 %collective-permute-start.1 = (bf16[32,384]{1,0:T(8,128)(2,1)S(1)}, bf16[32,384]{1,0:T(8,128)(2,1)S(1)}, u32[]{:S(2)}, u32[]{:S(2)}) collective-permute-start(bf16[32,384]{1,0:T(8,128)(2,1)S(1)} %pad_maximum_fusion.5), channel_id=1, source_target_pairs={{0,4},{1,5},{2,6},{3,7},{4,0},{5,1},{6,2},{7,3},{8,12},{9,13},{10,... | collective-permute-start | bytes 73736 | tf_op jit(solution)/shard_map/ppermute | solution.py:187
  15.4 4.1 %collective-permute-start.2 = (bf16[64,384]{1,0:T(8,128)(2,1)S(1)}, bf16[64,384]{1,0:T(8,128)(2,1)S(1)}, u32[]{:S(2)}, u32[]{:S(2)}) collective-permute-start(bf16[64,384]{1,0:T(8,128)(2,1)S(1)} %pad_maximum_fusion.4), channel_id=1, source_target_pairs={{0,2},{1,3},{2,0},{3,1},{4,6},{5,7},{6,4},{7,5},{8,10},{9,11},{10,... | collective-permute-start | bytes 147464 | tf_op jit(solution)/shard_map/ppermute | solution.py:187
  19.5 1.4 %collective-permute-start.3 = (bf16[128,384]{1,0:T(8,128)(2,1)S(1)}, bf16[128,384]{1,0:T(8,128)(2,1)S(1)}, u32[]{:S(2)}, u32[]{:S(2)}) collective-permute-start(bf16[128,384]{1,0:T(8,128)(2,1)S(1)} %pad_maximum_fusion.2), channel_id=1, source_target_pairs={{0,1},{1,0},{2,3},{3,2},{4,5},{5,4},{6,7},{7,6},{8,9},{9,8},{10,11... | collective-permute-start | bytes 294920 | tf_op jit(solution)/shard_map/ppermute | solution.py:187
  20.9 26.4 %copy-start = (bf16[48,16384]{1,0:T(8,128)(2,1)S(1)}, bf16[48,16384]{1,0:T(8,128)(2,1)}, u32[]{:S(2)}) copy-start(bf16[48,16384]{1,0:T(8,128)(2,1)} %stored.1) | copy-start | bytes 4718596
  20.9 26.3 %copy-start.2 = (s32[1,48]{1,0:T(1,128)S(1)}, s32[1,48]{1,0:T(1,128)}, u32[]{:S(2)}) copy-start(s32[1,48]{1,0:T(1,128)} %ids.1) | copy-start | bytes 580
  31.2 4.8 %collective-permute-start.4 = (bf16[1,16,1024]{2,1,0:T(8,128)(2,1)S(1)}, bf16[1,16,1024]{2,1,0:T(8,128)(2,1)S(1)}, u32[]{:S(2)}, u32[]{:S(2)}) collective-permute-start(bf16[1,16,1024]{2,1,0:T(8,128)(2,1)S(1)} %bitcast.4), channel_id=1, source_target_pairs={{0,8},{1,9},{2,10},{3,11},{4,12},{5,13},{6,14},{7,15},{8,0},{9,1},... | collective-permute-start | bytes 98312 | tf_op jit(solution)/shard_map/ppermute | solution.py:187
  36.1 4.3 %collective-permute-start.5 = (bf16[2,16,1024]{2,1,0:T(8,128)(2,1)S(1)}, bf16[2,16,1024]{2,1,0:T(8,128)(2,1)S(1)}, u32[]{:S(2)}, u32[]{:S(2)}) collective-permute-start(bf16[2,16,1024]{2,1,0:T(8,128)(2,1)S(1)} %pad_maximum_fusion.3), channel_id=1, source_target_pairs={{0,4},{1,5},{2,6},{3,7},{4,0},{5,1},{6,2},{7,3},{8,12},{9,13},{10,... | collective-permute-start | bytes 196616 | tf_op jit(solution)/shard_map/ppermute | solution.py:187
  40.4 5.2 %collective-permute-start.6 = (bf16[4,16,1024]{2,1,0:T(8,128)(2,1)S(1)}, bf16[4,16,1024]{2,1,0:T(8,128)(2,1)S(1)}, u32[]{:S(2)}, u32[]{:S(2)}) collective-permute-start(bf16[4,16,1024]{2,1,0:T(8,128)(2,1)S(1)} %pad_maximum_fusion.1), channel_id=1, source_target_pairs={{0,2},{1,3},{2,0},{3,1},{4,6},{5,7},{6,4},{7,5},{8,10},{9,11},{10,... | collective-permute-start | bytes 393224 | tf_op jit(solution)/shard_map/ppermute | solution.py:187
  45.7 1.6 %collective-permute-start.7 = (bf16[8,16,1024]{2,1,0:T(8,128)(2,1)S(1)}, bf16[8,16,1024]{2,1,0:T(8,128)(2,1)S(1)}, u32[]{:S(2)}, u32[]{:S(2)}) collective-permute-start(bf16[8,16,1024]{2,1,0:T(8,128)(2,1)S(1)} %pad_maximum_fusion.near), channel_id=1, source_target_pairs={{0,1},{1,0},{2,3},{3,2},{4,5},{5,4},{6,7},{7,6},{8,9},{9,8},{10,11... | collective-permute-start | bytes 786440 | tf_op jit(solution)/shard_map/ppermute | solution.py:187

commit v3 on v2

v3 whole, which is shorter than its diff:
```python
import functools

import jax
import jax.numpy as jnp
from jax import lax
from jax.experimental import pallas as pl
from jax.experimental.pallas import tpu as pltpu
from jax.sharding import PartitionSpec as P

LANES = 128
QRY_DEV = 1
EX_DEV = 16
NT = (((1,), (1,)), ((), ()))
VMEM = pl.BlockSpec(memory_space=pltpu.VMEM)
ANY = pl.BlockSpec(memory_space=pl.ANY)
VMEM_BYTES = 67_043_328 - (3 << 15)


def chunk_of(total, most):
    size = most
    while total % size:
        size //= 2
    return size


def round_up(n, m):
    return -(-n // m) * m


def taper(total, parts):
    tiles = total // LANES
    sizes = []
    for left in range(parts, 0, -1):
        size = tiles if left == 1 else -(-2 * tiles // (left + 1))
        sizes.append(size * LANES)
        tiles -= size
    return [size for size in sizes if size]


def project_kernel(acts, grads, in_w, out_w, raw, acts_v, grads_v, in_v, out_v, sem, *, sizes):
    pieces = [(grads, grads_v, out_w, out_v, 0, grads.shape[1])]
    for n, size in enumerate(sizes):
        pieces.append((acts, acts_v, in_w, in_v, sum(sizes[:n]), size))
    copies = []
    for n, (x, x_v, w, w_v, k, size) in enumerate(pieces):
        cols = pl.ds(k, size)
        copies.append(
            (
                pltpu.make_async_copy(x.at[:, cols], x_v.at[:, cols], sem.at[n, 0]),
                pltpu.make_async_copy(w.at[:, cols], w_v.at[:, cols], sem.at[n, 1]),
            )
        )
    for pair in copies:
        for copy in pair:
            copy.start()
    kin = in_w.shape[0]
    total = None
    for n, (x, x_v, w, w_v, k, size) in enumerate(pieces):
        for copy in copies[n]:
            copy.wait()
        part = lax.dot_general(
            x_v[:, k : k + size], w_v[:, k : k + size], NT, preferred_element_type=jnp.float32
        )
        if n == 0:
            raw[:, kin:] = part.astype(jnp.bfloat16)
        else:
            total = part if total is None else total + part
    raw[:, :kin] = total.astype(jnp.bfloat16)


def mark_kernel(raw, ids, tok):
    tokens, done = raw.shape
    row = lax.broadcasted_iota(jnp.int32, (tokens, tokens), 0)
    col = lax.broadcasted_iota(jnp.int32, (tokens, tokens), 1)
    mine = jnp.sum(jnp.where(row == col, ids[...], 0), axis=1, keepdims=True)
    query = lax.broadcasted_iota(jnp.int32, (tokens, tok.shape[1] - done), 1)
    tok[:, :done] = raw[...]
    tok[:, done:] = jnp.where(query == mine, 1.0, 0.0).astype(jnp.bfloat16)


def project(acts, grads, in_w, out_w, ids, queries):
    tokens, ff = acts.shape
    sizes = taper(ff, 5)
    width = in_w.shape[0] + out_w.shape[0]
    raw = pl.pallas_call(
        functools.partial(project_kernel, sizes=sizes),
        in_specs=[ANY] * 4,
        out_specs=VMEM,
        out_shape=jax.ShapeDtypeStruct((tokens, width), jnp.bfloat16),
        scratch_shapes=[
            pltpu.VMEM(acts.shape, acts.dtype),
            pltpu.VMEM(grads.shape, grads.dtype),
            pltpu.VMEM(in_w.shape, in_w.dtype),
            pltpu.VMEM(out_w.shape, out_w.dtype),
            pltpu.SemaphoreType.DMA((len(sizes) + 1, 2)),
        ],
        compiler_params=pltpu.CompilerParams(vmem_limit_bytes=VMEM_BYTES),
        name="project",
    )(acts, grads, in_w, out_w)
    return pl.pallas_call(
        mark_kernel,
        in_specs=[VMEM, VMEM],
        out_specs=VMEM,
        out_shape=jax.ShapeDtypeStruct(
            (tokens, width + round_up(queries, LANES)), jnp.bfloat16
        ),
        compiler_params=pltpu.CompilerParams(vmem_limit_bytes=2 << 20),
        cost_estimate=pl.CostEstimate(
            flops=10**11, bytes_accessed=10**8, transcendentals=0
        ),
        name="mark",
    )(raw, ids)


def precond_kernel(tok, inverse, out, out_t, member_t, *acc, kin, kout, per, fold, queries):
    out_t[...] = tok[:, kin : kin + kout].astype(jnp.float32).T.astype(jnp.bfloat16)
    member_t[...] = (
        tok[:, kin + kout :].astype(jnp.float32).T[:queries].astype(jnp.bfloat16)
    )

    def grads(first):
        o = out_t[pl.ds(first, per), :]
        weighted = (o[:, None, :] * member_t[...][None, :, :]).reshape(per * queries, o.shape[1])
        g = jnp.dot(weighted, tok[:, :kin], preferred_element_type=jnp.float32)
        g = g.astype(jnp.bfloat16)
        return [g[k * queries : (k + 1) * queries] for k in range(per)]

    def product(first):
        g = []
        for n in range(fold):
            g += grads(first + n * per)
        start = first * kin if isinstance(first, int) else pl.multiple_of(first * kin, kin)
        block = inverse[:, pl.ds(start, fold * per * kin)]
        return lax.dot_general(
            jnp.concatenate(g, axis=1), block, NT, preferred_element_type=jnp.float32
        )

    if not acc:
        out[...] = product(0).astype(jnp.bfloat16)
        return
    total = acc[0]
    total[...] = jnp.zeros_like(total)

    def step(s):
        total[...] += product(s * (fold * per))

    pl.loop(0, kout // (fold * per))(step)
    out[...] = total[...].astype(jnp.bfloat16)


def precondition(tok, inverse, kin, kout, queries):
    rows, coords = inverse.shape
    tokens = tok.shape[0]
    per = chunk_of(kout, max(8, (1 << 16) // (queries * tokens)))
    fold = chunk_of(kout // per, max(1, (1 << 18) // (per * queries * tokens) * 2))
    scratch = [
        pltpu.VMEM((kout, tokens), jnp.bfloat16),
        pltpu.VMEM((queries, tokens), jnp.bfloat16),
    ]
    if fold * per < kout:
        scratch.append(pltpu.VMEM((queries, rows), jnp.float32))
    return pl.pallas_call(
        functools.partial(
            precond_kernel, kin=kin, kout=kout, per=per, fold=fold, queries=queries
        ),
        in_specs=[VMEM, VMEM],
        out_specs=VMEM,
        out_shape=jax.ShapeDtypeStruct((queries, rows), jnp.bfloat16),
        scratch_shapes=scratch,
        compiler_params=pltpu.CompilerParams(vmem_limit_bytes=16 << 20),
        cost_estimate=pl.CostEstimate(
            flops=2 * queries * rows * coords,
            bytes_accessed=2 * rows * coords,
            transcendentals=0,
        ),
        name="precondition",
    )(tok, inverse)


def block_scores(blocks, stored, masks, axis):
    me = lax.axis_index(axis)
    rows = blocks.shape[2]
    scores = jnp.zeros((stored.shape[0], blocks.shape[1]), jnp.float32)
    for n, mask in enumerate(masks):
        start = pl.multiple_of((me ^ mask) * rows, rows)
        scores += lax.dot_general(
            stored[:, pl.ds(start, rows)], blocks[n], NT, preferred_element_type=jnp.float32
        )
    return scores


def near_kernel(near, stored, part, *, masks, axis):
    part[...] = block_scores(near, stored, masks, axis)


def far_kernel(far, part, stored, ids, out, *, masks, axis):
    scores = part[...] + block_scores(far, stored, masks, axis)
    example = lax.broadcasted_iota(jnp.int32, (out.shape[0], ids.shape[1]), 0)
    member = jnp.where(example == ids[...], 1.0, 0.0)
    out[...] = jnp.dot(
        member, scores, precision=lax.Precision.HIGHEST, preferred_element_type=jnp.float32
    )


def score_cost(stored, queries):
    return pl.CostEstimate(
        flops=stored.size * queries, bytes_accessed=stored.size, transcendentals=0
    )


def score_near(near, stored, masks, queries):
    return pl.pallas_call(
        functools.partial(near_kernel, masks=masks, axis="rows"),
        in_specs=[VMEM] * 2,
        out_specs=VMEM,
        out_shape=jax.ShapeDtypeStruct((stored.shape[0], queries), jnp.float32),
        compiler_params=pltpu.CompilerParams(vmem_limit_bytes=8 << 20),
        cost_estimate=score_cost(stored, queries),
        name="score_near",
    )(near, stored)


def score_far(far, part, stored, ids, masks, queries):
    return pl.pallas_call(
        functools.partial(far_kernel, masks=masks, axis="rows"),
        in_specs=[VMEM] * 4,
        out_specs=VMEM,
        out_shape=jax.ShapeDtypeStruct((EX_DEV, queries), jnp.float32),
        compiler_params=pltpu.CompilerParams(vmem_limit_bytes=8 << 20),
        cost_estimate=score_cost(stored, queries),
        name="score_far",
    )(far, part, stored, ids)


def stages_of(n, crossed):
    masks = []
    bit = n // 2
    while bit:
        masks.append(bit | 1 if len(masks) < crossed else bit)
        bit //= 2
    return masks


def swap(x, mask, n):
    return lax.ppermute(x, "rows", [(i, i ^ mask) for i in range(n)])


def on_device(
    in_acts, out_grads, in_projection, out_projection, inverse, stored_rows, query_ids, example_ids
):
    n = lax.axis_size("rows")
    queries = QRY_DEV * n
    kin, kout = in_projection.shape[0], out_projection.shape[0]
    tok = project(
        in_acts, out_grads, in_projection, out_projection, query_ids[None, :], queries
    )
    for mask in stages_of(n, n):
        tok = jnp.concatenate([tok, swap(tok, mask, n)], axis=0)
    near = precondition(tok, inverse, kin, kout, queries)[None]
    held = [0]
    *stages, last = stages_of(n, 1)
    for mask in stages:
        held += [m ^ mask for m in held]
        near = jnp.concatenate([near, swap(near, mask, n)], axis=0)
    far = swap(near, last, n)
    part = score_near(near, stored_rows, held, queries)
    return score_far(far, part, stored_rows, example_ids, [m ^ last for m in held], queries)


def solution(mesh):
    placed = (
        P(("groups", "rows"), None),
        P(("groups", "rows"), None),
        P(),
        P(),
        P("rows", None),
        P(("groups", "rows"), None),
        P(("groups", "rows")),
        P(("groups", "rows"), None),
    )
    return jax.shard_map(
        on_device,
        mesh=mesh,
        in_specs=placed,
        out_specs=P(("groups", "rows"), None),
        check_vma=False,
    )
```

time: 48.8 us -> 45.1 us (0.924)
  waiting for transfers between devices: 15.8 us -> 14.2 us
  Pallas kernels: 16.4 us -> 15 us
  starting transfers between devices: 15.2 us -> 14.4 us
    ppermute x8, waiting for transfers between devices: 15.8 us -> 14.2 us  [swap(): return lax.ppermute(x, 'rows', [(i, i ^ mask) for i in range(n)])]
    pallas_call x1, Pallas kernels: 10.3 us -> 9.05 us  [precondition(): pl.pallas_call(functools.partial(precond_kernel, kin=kin, kout=kout, per=...]
    ppermute x8, starting transfers between devices: 15.2 us -> 14.4 us  [swap(): return lax.ppermute(x, 'rows', [(i, i ^ mask) for i in range(n)])]
    pallas_call x2 -> x3, Pallas kernels: 6.07 us -> 5.91 us  [the longest x1 4.46 us: project(): pl.pallas_call(functools.partial(project_kernel, sizes=sizes), in_specs=[...]
  transfers between devices with their start and end apart: 8 -> 8, of which waited for: 8 -> 8; matrix products, arithmetic and copies ran while one was open for 0% -> 0% of each run, Pallas kernels for 0% -> 1%
where the time goes in v3:
time: 45.1 us; the launch traced here: 44.9 us
  Pallas kernels  15 us (33%)
  starting transfers between devices  14.4 us (32%)
  waiting for transfers between devices  14.2 us (31%)
  local copies, waits for them, and re-layouts  0.94 us (2%)
    ppermute x8, starting transfers between devices, swap(): return lax.ppermute(x, 'rows', [(i, i ^ mask) for i in range(n)])  14.4 us
    ppermute x8, waiting for transfers between devices, swap(): return lax.ppermute(x, 'rows', [(i, i ^ mask) for i in range(n)])  14.2 us
    pallas_call x1, Pallas kernels, precondition(): pl.pallas_call(functools.partial(precond_kernel, kin=kin, kout=kout, per=...  9.05 us
    pallas_call x1, Pallas kernels, project(): pl.pallas_call(functools.partial(project_kernel, sizes=sizes), in_specs=[...  4.46 us
    pallas_call x1, Pallas kernels, score_far(): pl.pallas_call(functools.partial(far_kernel, masks=masks, axis='rows'), i...  1.1 us
    unnamed x28, local copies, waits for them, and re-layouts  0.93 us
  transfers between devices with their start and end apart: 8, of which 8 were waited for; matrix products, arithmetic and copies ran while one was open for 0% of the time, Pallas kernels for 1%

profile of v3, /device:TPU:0, one launch (start us, length us, event | category | flops | bytes accessed | tf_op | source)
XLA Modules:
  0.0 44.9 jit_solution(7875365544487232513)
XLA Ops:
  0.0 4.5 %project.1.raw = bf16[16,256]{1,0:T(8,128)(2,1)} custom-call(bf16[16,14336]{1,0:T(8,128)(2,1)} %acts.1, bf16[16,4096]{1,0:T(8,128)(2,1)} %grads.1, bf16[128,14336]{1,0:T(8,128)(2,1)} %in_w.1, bf16[128,4096]{1,0:T(8,128)(2,1)} %out_w.1), custom_call_target="tpu_custom_call" | custom-call | tf_op jit(solution)/shard_map/project/pallas_call | solution.py:85
  4.5 0.0 slice-start
  4.5 0.8 %copy-done.1 = bf16[16,256]{1,0:T(8,128)(2,1)S(1)} copy-done((bf16[16,256]{1,0:T(8,128)(2,1)S(1)}, bf16[16,256]{1,0:T(8,128)(2,1)}, u32[]{:S(2)}) %copy-start.1) | copy-done | bytes 8216
  5.4 0.1 mark.1
  5.5 3.5 %collective-permute-start = (bf16[16,384]{1,0:T(8,128)(2,1)S(1)}, bf16[16,384]{1,0:T(8,128)(2,1)S(1)}, u32[]{:S(2)}, u32[]{:S(2)}) collective-permute-start(bf16[16,384]{1,0:T(8,128)(2,1)S(1)} %mark.1), channel_id=1, source_target_pairs={{0,9},{1,8},{2,11},{3,10},{4,13},{5,12},{6,15},{7,14},{8,1},{9,0},... | collective-permute-start | bytes 36872 | tf_op jit(solution)/shard_map/ppermute | solution.py:245
  9.0 1.4 %collective-permute-done = bf16[16,384]{1,0:T(8,128)(2,1)S(1)} collective-permute-done((bf16[16,384]{1,0:T(8,128)(2,1)S(1)}, bf16[16,384]{1,0:T(8,128)(2,1)S(1)}, u32[]{:S(2)}, u32[]{:S(2)}) %collective-permute-start) | collective-permute-done | bytes 12320 | tf_op jit(solution)/shard_map/ppermute | solution.py:245
  10.4 1.9 %collective-permute-start.1 = (bf16[32,384]{1,0:T(8,128)(2,1)S(1)}, bf16[32,384]{1,0:T(8,128)(2,1)S(1)}, u32[]{:S(2)}, u32[]{:S(2)}) collective-permute-start(bf16[32,384]{1,0:T(8,128)(2,1)S(1)} %pad_maximum_fusion.5), channel_id=1, source_target_pairs={{0,5},{1,4},{2,7},{3,6},{4,1},{5,0},{6,3},{7,2},{8,13},{9,12},{10,... | collective-permute-start | bytes 73736 | tf_op jit(solution)/shard_map/ppermute | solution.py:245
  12.3 1.5 %collective-permute-done.1 = bf16[32,384]{1,0:T(8,128)(2,1)S(1)} collective-permute-done((bf16[32,384]{1,0:T(8,128)(2,1)S(1)}, bf16[32,384]{1,0:T(8,128)(2,1)S(1)}, u32[]{:S(2)}, u32[]{:S(2)}) %collective-permute-start.1) | collective-permute-done | bytes 24608 | tf_op jit(solution)/shard_map/ppermute | solution.py:245
  13.8 1.7 %collective-permute-start.2 = (bf16[64,384]{1,0:T(8,128)(2,1)S(1)}, bf16[64,384]{1,0:T(8,128)(2,1)S(1)}, u32[]{:S(2)}, u32[]{:S(2)}) collective-permute-start(bf16[64,384]{1,0:T(8,128)(2,1)S(1)} %pad_maximum_fusion.4), channel_id=1, source_target_pairs={{0,3},{1,2},{2,1},{3,0},{4,7},{5,6},{6,5},{7,4},{8,11},{9,10},{10,... | collective-permute-start | bytes 147464 | tf_op jit(solution)/shard_map/ppermute | solution.py:245
  15.5 1.8 %collective-permute-done.2 = bf16[64,384]{1,0:T(8,128)(2,1)S(1)} collective-permute-done((bf16[64,384]{1,0:T(8,128)(2,1)S(1)}, bf16[64,384]{1,0:T(8,128)(2,1)S(1)}, u32[]{:S(2)}, u32[]{:S(2)}) %collective-permute-start.2) | collective-permute-done | bytes 49184 | tf_op jit(solution)/shard_map/ppermute | solution.py:245
  17.3 0.6 %collective-permute-start.3 = (bf16[128,384]{1,0:T(8,128)(2,1)S(1)}, bf16[128,384]{1,0:T(8,128)(2,1)S(1)}, u32[]{:S(2)}, u32[]{:S(2)}) collective-permute-start(bf16[128,384]{1,0:T(8,128)(2,1)S(1)} %pad_maximum_fusion.2), channel_id=1, source_target_pairs={{0,1},{1,0},{2,3},{3,2},{4,5},{5,4},{6,7},{7,6},{8,9},{9,8},{10,11... | collective-permute-start | bytes 294920 | tf_op jit(solution)/shard_map/ppermute | solution.py:245
  17.9 0.9 %collective-permute-done.3 = bf16[128,384]{1,0:T(8,128)(2,1)S(1)} collective-permute-done((bf16[128,384]{1,0:T(8,128)(2,1)S(1)}, bf16[128,384]{1,0:T(8,128)(2,1)S(1)}, u32[]{:S(2)}, u32[]{:S(2)}) %collective-permute-start.3) | collective-permute-done | bytes 98336 | tf_op jit(solution)/shard_map/ppermute | solution.py:245
  19.0 0.0 copy-start
  19.0 9.0 %precondition.1 = bf16[16,1024]{1,0:T(8,128)(2,1)S(1)} custom-call(bf16[256,384]{1,0:T(8,128)(2,1)S(1)} %constant_dynamic-update-slice_fusion.tok, bf16[1024,16384]{1,0:T(8,128)(2,1)S(1)} %bitcast.3), custom_call_target="tpu_custom_call" | custom-call | flops 536870912 | bytes 33554432 | tf_op jit(solution)/shard_map/precondition/pallas_call | solution.py:162
  28.0 3.0 %collective-permute-start.4 = (bf16[1,16,1024]{2,1,0:T(8,128)(2,1)S(1)}, bf16[1,16,1024]{2,1,0:T(8,128)(2,1)S(1)}, u32[]{:S(2)}, u32[]{:S(2)}) collective-permute-start(bf16[1,16,1024]{2,1,0:T(8,128)(2,1)S(1)} %bitcast.4), channel_id=1, source_target_pairs={{0,9},{1,8},{2,11},{3,10},{4,13},{5,12},{6,15},{7,14},{8,1},{9,0},... | collective-permute-start | bytes 98312 | tf_op jit(solution)/shard_map/ppermute | solution.py:245
  31.0 1.6 %collective-permute-done.4 = bf16[1,16,1024]{2,1,0:T(8,128)(2,1)S(1)} collective-permute-done((bf16[1,16,1024]{2,1,0:T(8,128)(2,1)S(1)}, bf16[1,16,1024]{2,1,0:T(8,128)(2,1)S(1)}, u32[]{:S(2)}, u32[]{:S(2)}) %collective-permute-start.4) | collective-permute-done | bytes 32800 | tf_op jit(solution)/shard_map/ppermute | solution.py:245
  32.7 2.0 %collective-permute-start.5 = (bf16[2,16,1024]{2,1,0:T(8,128)(2,1)S(1)}, bf16[2,16,1024]{2,1,0:T(8,128)(2,1)S(1)}, u32[]{:S(2)}, u32[]{:S(2)}) collective-permute-start(bf16[2,16,1024]{2,1,0:T(8,128)(2,1)S(1)} %pad_maximum_fusion.3), channel_id=1, source_target_pairs={{0,4},{1,5},{2,6},{3,7},{4,0},{5,1},{6,2},{7,3},{8,12},{9,13},{10,... | collective-permute-start | bytes 196616 | tf_op jit(solution)/shard_map/ppermute | solution.py:245
  34.7 2.4 %collective-permute-done.5 = bf16[2,16,1024]{2,1,0:T(8,128)(2,1)S(1)} collective-permute-done((bf16[2,16,1024]{2,1,0:T(8,128)(2,1)S(1)}, bf16[2,16,1024]{2,1,0:T(8,128)(2,1)S(1)}, u32[]{:S(2)}, u32[]{:S(2)}) %collective-permute-start.5) | collective-permute-done | bytes 65568 | tf_op jit(solution)/shard_map/ppermute | solution.py:245
  37.1 1.7 %collective-permute-start.6 = (bf16[4,16,1024]{2,1,0:T(8,128)(2,1)S(1)}, bf16[4,16,1024]{2,1,0:T(8,128)(2,1)S(1)}, u32[]{:S(2)}, u32[]{:S(2)}) collective-permute-start(bf16[4,16,1024]{2,1,0:T(8,128)(2,1)S(1)} %pad_maximum_fusion.1), channel_id=1, source_target_pairs={{0,2},{1,3},{2,0},{3,1},{4,6},{5,7},{6,4},{7,5},{8,10},{9,11},{10,... | collective-permute-start | bytes 393224 | tf_op jit(solution)/shard_map/ppermute | solution.py:245
  38.8 3.4 %collective-permute-done.6 = bf16[4,16,1024]{2,1,0:T(8,128)(2,1)S(1)} collective-permute-done((bf16[4,16,1024]{2,1,0:T(8,128)(2,1)S(1)}, bf16[4,16,1024]{2,1,0:T(8,128)(2,1)S(1)}, u32[]{:S(2)}, u32[]{:S(2)}) %collective-permute-start.6) | collective-permute-done | bytes 131104 | tf_op jit(solution)/shard_map/ppermute | solution.py:245
  42.2 0.1 collective-permute-start.7
  42.2 0.3 score_near.1.part
  42.6 1.2 %collective-permute-done.7.far = bf16[8,16,1024]{2,1,0:T(8,128)(2,1)S(1)} collective-permute-done((bf16[8,16,1024]{2,1,0:T(8,128)(2,1)S(1)}, bf16[8,16,1024]{2,1,0:T(8,128)(2,1)S(1)}, u32[]{:S(2)}, u32[]{:S(2)}) %collective-permute-start.7) | collective-permute-done | bytes 262176 | tf_op jit(solution)/shard_map/ppermute | solution.py:245
  43.8 1.1 %score_far.1 = f32[16,16]{1,0:T(8,128)} custom-call(bf16[8,16,1024]{2,1,0:T(8,128)(2,1)S(1)} %collective-permute-done.7.far, f32[48,16]{1,0:T(8,128)S(1)} %score_near.1.part, bf16[48,16384]{1,0:T(8,128)(2,1)S(1)} %copy-done, s32[1,48]{1,0:T(1,128)S(1)} %copy-done.2), custom_call_target="tpu_custom_call" | custom-call | flops 12582912 | bytes 786432 | tf_op jit(solution)/shard_map/score_far/pallas_call | solution.py:224
  (33 shorter events, 0.2 us)
Async XLA Ops:
  0.0 4.5 %copy-start.3 = (s32[16]{0:T(128)S(1)}, s32[16]{0:T(128)}, u32[]{:S(2)}) copy-start(s32[16]{0:T(128)} %param.14) | copy-start | bytes 196
  4.5 14.4 %slice-start = ((s8[33554432]{0:T(1024)(128)(4,1)}), s8[4194304]{0:T(1024)(128)(4,1)S(1)}, s32[]{:S(2)}) async-start(s8[33554432]{0:T(1024)(128)(4,1)} %bitcast.2), calls=%async_computation | async-start | bytes 8388608
  4.5 0.8 %copy-start.1 = (bf16[16,256]{1,0:T(8,128)(2,1)S(1)}, bf16[16,256]{1,0:T(8,128)(2,1)}, u32[]{:S(2)}) copy-start(bf16[16,256]{1,0:T(8,128)(2,1)} %project.1.raw) | copy-start | bytes 24580
  5.3 13.5 %slice-start.1 = ((s8[33554432]{0:T(1024)(128)(4,1)}), s8[4194304]{0:T(1024)(128)(4,1)S(1)}, s32[]{:S(2)}) async-start(s8[33554432]{0:T(1024)(128)(4,1)} %bitcast.2), calls=%async_computation.1 | async-start | bytes 8388608
  5.3 13.5 %slice-start.2 = ((s8[33554432]{0:T(1024)(128)(4,1)}), s8[4194304]{0:T(1024)(128)(4,1)S(1)}, s32[]{:S(2)}) async-start(s8[33554432]{0:T(1024)(128)(4,1)} %bitcast.2), calls=%async_computation.2 | async-start | bytes 8388608
  5.4 13.5 %slice-start.3 = ((s8[33554432]{0:T(1024)(128)(4,1)}), s8[4194304]{0:T(1024)(128)(4,1)S(1)}, s32[]{:S(2)}) async-start(s8[33554432]{0:T(1024)(128)(4,1)} %bitcast.2), calls=%async_computation.3 | async-start | bytes 8388608
  5.4 13.6 %slice-start.4 = ((s8[33554432]{0:T(1024)(128)(4,1)}), s8[4194304]{0:T(1024)(128)(4,1)S(1)}, s32[]{:S(2)}) async-start(s8[33554432]{0:T(1024)(128)(4,1)} %bitcast.2), calls=%async_computation.4 | async-start | bytes 8388608
  5.4 13.6 %slice-start.5 = ((s8[33554432]{0:T(1024)(128)(4,1)}), s8[4194304]{0:T(1024)(128)(4,1)S(1)}, s32[]{:S(2)}) async-start(s8[33554432]{0:T(1024)(128)(4,1)} %bitcast.2), calls=%async_computation.5 | async-start | bytes 8388608
  5.4 13.6 %slice-start.6 = ((s8[33554432]{0:T(1024)(128)(4,1)}), s8[4194304]{0:T(1024)(128)(4,1)S(1)}, s32[]{:S(2)}) async-start(s8[33554432]{0:T(1024)(128)(4,1)} %bitcast.2), calls=%async_computation.6 | async-start | bytes 8388608
  5.4 13.6 %slice-start.7 = ((s8[33554432]{0:T(1024)(128)(4,1)}), s8[4194304]{0:T(1024)(128)(4,1)S(1)}, s32[]{:S(2)}) async-start(s8[33554432]{0:T(1024)(128)(4,1)} %bitcast.2), calls=%async_computation.7 | async-start | bytes 8388608
  5.5 4.9 %collective-permute-start = (bf16[16,384]{1,0:T(8,128)(2,1)S(1)}, bf16[16,384]{1,0:T(8,128)(2,1)S(1)}, u32[]{:S(2)}, u32[]{:S(2)}) collective-permute-start(bf16[16,384]{1,0:T(8,128)(2,1)S(1)} %mark.1), channel_id=1, source_target_pairs={{0,9},{1,8},{2,11},{3,10},{4,13},{5,12},{6,15},{7,14},{8,1},{9,0},... | collective-permute-start | bytes 36872 | tf_op jit(solution)/shard_map/ppermute | solution.py:245
  10.4 3.4 %collective-permute-start.1 = (bf16[32,384]{1,0:T(8,128)(2,1)S(1)}, bf16[32,384]{1,0:T(8,128)(2,1)S(1)}, u32[]{:S(2)}, u32[]{:S(2)}) collective-permute-start(bf16[32,384]{1,0:T(8,128)(2,1)S(1)} %pad_maximum_fusion.5), channel_id=1, source_target_pairs={{0,5},{1,4},{2,7},{3,6},{4,1},{5,0},{6,3},{7,2},{8,13},{9,12},{10,... | collective-permute-start | bytes 73736 | tf_op jit(solution)/shard_map/ppermute | solution.py:245
  13.8 3.5 %collective-permute-start.2 = (bf16[64,384]{1,0:T(8,128)(2,1)S(1)}, bf16[64,384]{1,0:T(8,128)(2,1)S(1)}, u32[]{:S(2)}, u32[]{:S(2)}) collective-permute-start(bf16[64,384]{1,0:T(8,128)(2,1)S(1)} %pad_maximum_fusion.4), channel_id=1, source_target_pairs={{0,3},{1,2},{2,1},{3,0},{4,7},{5,6},{6,5},{7,4},{8,11},{9,10},{10,... | collective-permute-start | bytes 147464 | tf_op jit(solution)/shard_map/ppermute | solution.py:245
  17.3 1.5 %collective-permute-start.3 = (bf16[128,384]{1,0:T(8,128)(2,1)S(1)}, bf16[128,384]{1,0:T(8,128)(2,1)S(1)}, u32[]{:S(2)}, u32[]{:S(2)}) collective-permute-start(bf16[128,384]{1,0:T(8,128)(2,1)S(1)} %pad_maximum_fusion.2), channel_id=1, source_target_pairs={{0,1},{1,0},{2,3},{3,2},{4,5},{5,4},{6,7},{7,6},{8,9},{9,8},{10,11... | collective-permute-start | bytes 294920 | tf_op jit(solution)/shard_map/ppermute | solution.py:245
  19.0 23.3 %copy-start = (bf16[48,16384]{1,0:T(8,128)(2,1)S(1)}, bf16[48,16384]{1,0:T(8,128)(2,1)}, u32[]{:S(2)}) copy-start(bf16[48,16384]{1,0:T(8,128)(2,1)} %stored.3) | copy-start | bytes 4718596
  19.0 24.8 %copy-start.2 = (s32[1,48]{1,0:T(1,128)S(1)}, s32[1,48]{1,0:T(1,128)}, u32[]{:S(2)}) copy-start(s32[1,48]{1,0:T(1,128)} %ids.1) | copy-start | bytes 580
  28.0 4.6 %collective-permute-start.4 = (bf16[1,16,1024]{2,1,0:T(8,128)(2,1)S(1)}, bf16[1,16,1024]{2,1,0:T(8,128)(2,1)S(1)}, u32[]{:S(2)}, u32[]{:S(2)}) collective-permute-start(bf16[1,16,1024]{2,1,0:T(8,128)(2,1)S(1)} %bitcast.4), channel_id=1, source_target_pairs={{0,9},{1,8},{2,11},{3,10},{4,13},{5,12},{6,15},{7,14},{8,1},{9,0},... | collective-permute-start | bytes 98312 | tf_op jit(solution)/shard_map/ppermute | solution.py:245
  32.7 4.4 %collective-permute-start.5 = (bf16[2,16,1024]{2,1,0:T(8,128)(2,1)S(1)}, bf16[2,16,1024]{2,1,0:T(8,128)(2,1)S(1)}, u32[]{:S(2)}, u32[]{:S(2)}) collective-permute-start(bf16[2,16,1024]{2,1,0:T(8,128)(2,1)S(1)} %pad_maximum_fusion.3), channel_id=1, source_target_pairs={{0,4},{1,5},{2,6},{3,7},{4,0},{5,1},{6,2},{7,3},{8,12},{9,13},{10,... | collective-permute-start | bytes 196616 | tf_op jit(solution)/shard_map/ppermute | solution.py:245
  37.1 5.0 %collective-permute-start.6 = (bf16[4,16,1024]{2,1,0:T(8,128)(2,1)S(1)}, bf16[4,16,1024]{2,1,0:T(8,128)(2,1)S(1)}, u32[]{:S(2)}, u32[]{:S(2)}) collective-permute-start(bf16[4,16,1024]{2,1,0:T(8,128)(2,1)S(1)} %pad_maximum_fusion.1), channel_id=1, source_target_pairs={{0,2},{1,3},{2,0},{3,1},{4,6},{5,7},{6,4},{7,5},{8,10},{9,11},{10,... | collective-permute-start | bytes 393224 | tf_op jit(solution)/shard_map/ppermute | solution.py:245
  42.2 1.6 %collective-permute-start.7 = (bf16[8,16,1024]{2,1,0:T(8,128)(2,1)S(1)}, bf16[8,16,1024]{2,1,0:T(8,128)(2,1)S(1)}, u32[]{:S(2)}, u32[]{:S(2)}) collective-permute-start(bf16[8,16,1024]{2,1,0:T(8,128)(2,1)S(1)} %pad_maximum_fusion.near), channel_id=1, source_target_pairs={{0,1},{1,0},{2,3},{3,2},{4,5},{5,4},{6,7},{7,6},{8,9},{9,8},{10,11... | collective-permute-start | bytes 786440 | tf_op jit(solution)/shard_map/ppermute | solution.py:245
